TPU v7x, 256 devices: a whole 4x4x8 slice. The times are simulated.
256 devices in a mesh: blk: 32 (over x_lo, z, core), rep: 8 (over x_hi, y).
Axes of the slice: x: 4 (x_hi: 2, x_lo: 2; x = x_hi * 2 + x_lo), y: 4, z: 8, core: 2. Of those that a mesh axis runs over, the one named last changes fastest.
Arguments:
- integrals: bfloat16 [32, 512, 1024], P('blk'), may hold values from -0.59765625 to 0.59765625
- eps_occ: float32 [32], replicated, may hold values from -2 to -0.5
- eps_vir: float32 [512], replicated, may hold values from 0.5 to 3
- offsets: int32 [16], P('rep'), may hold values from 0 to 15
Outputs:
- gamma: float32 [32, 512, 1024], P('blk', None, 'rep')
All inputs are finite; a program needn't handle non-finite values.
Results may differ from a plain program's by a relative error of at most 0.0017.
Values may be sent and summed in bfloat16 or wider, within the bound.
A program may use at most 64 MiB of HBM per device.

v0:
```python
import jax
import jax.numpy as jnp
from jax import lax
from jax.sharding import PartitionSpec as P


def shifted(block, axis, distance):
    devices = range(lax.axis_size(axis))
    route = [((i - distance) % len(devices), i) for i in devices]
    return lax.ppermute(block, axis, route)


def walk_ahead(tile, offset):
    for level in range(lax.axis_size("blk").bit_length() - 2):
        moved = shifted(tile, "blk", 1 << level)
        tile = jnp.where(offset // (1 << level) % 2 == 1, moved, tile)
    return tile


def walk_back(tile, offset):
    for level in range(lax.axis_size("blk").bit_length() - 2):
        moved = shifted(tile, "blk", -(1 << level))
        tile = jnp.where(offset // (1 << level) % 2 == 1, moved, tile)
    return tile


def pair_amp(left, right, e_left, e_right, eps_vir):
    pair = lax.dot_general(
        left, right, (((1,), (1,)), ((), ())), preferred_element_type=jnp.float32
    )
    denom = eps_vir[:, None] + eps_vir[None, :] - e_left - e_right
    return (-pair / denom).astype(jnp.bfloat16)


def per_device(integrals, eps_occ, eps_vir, offsets):
    tile = integrals[0]
    occupied = eps_occ.shape[0]
    here = lax.axis_index("blk")
    e_here = lax.dynamic_index_in_dim(eps_occ, here, keepdims=False)
    total = jnp.zeros(tile.shape, jnp.float32)
    for slot in range(offsets.shape[0]):
        shift = offsets[slot]
        other = walk_ahead(tile, shift)
        e_other = lax.dynamic_index_in_dim(eps_occ, (here - shift) % occupied, keepdims=False)
        amp = pair_amp(tile, other, e_here, e_other, eps_vir)
        own = jnp.dot(amp, other, preferred_element_type=jnp.float32)
        part = lax.dot_general(
            amp, tile, (((0,), (0,)), ((), ())), preferred_element_type=jnp.float32
        )
        returned = walk_back(part.astype(jnp.bfloat16), shift)
        total = total + own + returned.astype(jnp.float32)
    gamma = lax.psum_scatter(total, "rep", scatter_dimension=1, tiled=True)
    return gamma[None]


def solution(mesh):
    in_specs = (P("blk", None, None), P(), P(), P("rep"))
    out_specs = P("blk", None, "rep")
    return jax.shard_map(
        per_device, mesh=mesh, in_specs=in_specs, out_specs=out_specs, check_vma=False
    )
```

profile of v0, /device:TPU:1, one launch (start us, length us, event | category | flops | bytes accessed | tf_op | source)
XLA Modules:
  0.0 630.1 jit_solution(15599285584600135255)
XLA Ops:
  6.5 3.0 collective-permute-start
  14.7 6.9 %collective-permute-done = bf16[512,1024]{1,0:T(8,128)(2,1)S(1)} collective-permute-done((bf16[512,1024]{1,0:T(8,128)(2,1)}, bf16[512,1024]{1,0:T(8,128)(2,1)S(1)}, u32[]{:S(2)}, u32[]{:S(2)}) %collective-permute-start) | collective-permute-done | bytes 1048608 | tf_op jit(solution)/shard_map/ppermute | solution.py:10
  27.0 19.1 %collective-permute-done.8 = bf16[512,1024]{1,0:T(8,128)(2,1)} collective-permute-done((bf16[512,1024]{1,0:T(8,128)(2,1)S(1)}, bf16[512,1024]{1,0:T(8,128)(2,1)}, u32[]{:S(2)}, u32[]{:S(2)}) %collective-permute-start.8) | collective-permute-done | bytes 1048608 | tf_op jit(solution)/shard_map/ppermute | solution.py:10
  46.3 5.7 collective-permute-start.9
  52.6 16.0 %collective-permute-done.1 = bf16[512,1024]{1,0:T(8,128)(2,1)} collective-permute-done((bf16[512,1024]{1,0:T(8,128)(2,1)S(1)}, bf16[512,1024]{1,0:T(8,128)(2,1)}, u32[]{:S(2)}, u32[]{:S(2)}) %collective-permute-start.1) | collective-permute-done | bytes 1048608 | tf_op jit(solution)/shard_map/ppermute | solution.py:10
  68.7 6.1 collective-permute-start.2
  74.9 37.0 %collective-permute-done.9 = bf16[512,1024]{1,0:T(8,128)(2,1)} collective-permute-done((bf16[512,1024]{1,0:T(8,128)(2,1)S(1)}, bf16[512,1024]{1,0:T(8,128)(2,1)}, u32[]{:S(2)}, u32[]{:S(2)}) %collective-permute-start.9) | collective-permute-done | bytes 1048608 | tf_op jit(solution)/shard_map/ppermute | solution.py:10
  112.0 6.6 %collective-permute-start.10 = (bf16[512,1024]{1,0:T(8,128)(2,1)S(1)}, bf16[512,1024]{1,0:T(8,128)(2,1)}, u32[]{:S(2)}, u32[]{:S(2)}) collective-permute-start(bf16[512,1024]{1,0:T(8,128)(2,1)S(1)} %broadcast_select_fusion.5), channel_id=1, source_target_pairs={{192,0},{200,8},{208,16},{216,24},{224,32},{232,40},{240,48},{248,... | collective-permute-start | bytes 3145736 | tf_op jit(solution)/shard_map/ppermute | solution.py:10
  118.7 33.6 %collective-permute-done.2 = bf16[512,1024]{1,0:T(8,128)(2,1)} collective-permute-done((bf16[512,1024]{1,0:T(8,128)(2,1)S(1)}, bf16[512,1024]{1,0:T(8,128)(2,1)}, u32[]{:S(2)}, u32[]{:S(2)}) %collective-permute-start.2) | collective-permute-done | bytes 1048608 | tf_op jit(solution)/shard_map/ppermute | solution.py:10
  153.6 9.8 %collective-permute-start.3 = (bf16[512,1024]{1,0:T(8,128)(2,1)S(1)}, bf16[512,1024]{1,0:T(8,128)(2,1)S(1)}, u32[]{:S(2)}, u32[]{:S(2)}) collective-permute-start(bf16[512,1024]{1,0:T(8,128)(2,1)S(1)} %broadcast_select_fusion.12), channel_id=1, source_target_pairs={{192,0},{200,8},{208,16},{216,24},{224,32},{232,40},{240,48},{248,... | collective-permute-start | bytes 3145736 | tf_op jit(solution)/shard_map/ppermute | solution.py:10
  165.4 22.6 %collective-permute-done.10 = bf16[512,1024]{1,0:T(8,128)(2,1)} collective-permute-done((bf16[512,1024]{1,0:T(8,128)(2,1)S(1)}, bf16[512,1024]{1,0:T(8,128)(2,1)}, u32[]{:S(2)}, u32[]{:S(2)}) %collective-permute-start.10) | collective-permute-done | bytes 1048608 | tf_op jit(solution)/shard_map/ppermute | solution.py:10
  188.1 3.3 fusion.5
  192.2 17.8 %collective-permute-start.11 = (bf16[512,1024]{1,0:T(8,128)(2,1)S(1)}, bf16[512,1024]{1,0:T(8,128)(2,1)S(1)}, u32[]{:S(2)}, u32[]{:S(2)}) collective-permute-start(bf16[512,1024]{1,0:T(8,128)(2,1)S(1)} %convolution_convert_fusion), channel_id=1, source_target_pairs={{8,0},{16,8},{24,16},{32,24},{40,32},{48,40},{56,48},{64,56},{72,6... | collective-permute-start | bytes 3145736 | tf_op jit(solution)/shard_map/ppermute | solution.py:10
  210.0 2.1 fusion.4
  212.8 49.4 %collective-permute-start.4 = (bf16[512,1024]{1,0:T(8,128)(2,1)S(1)}, bf16[512,1024]{1,0:T(8,128)(2,1)S(1)}, u32[]{:S(2)}, u32[]{:S(2)}) collective-permute-start(bf16[512,1024]{1,0:T(8,128)(2,1)S(1)} %convolution_convert_fusion.1), channel_id=1, source_target_pairs={{8,0},{16,8},{24,16},{32,24},{40,32},{48,40},{56,48},{64,56},{72,6... | collective-permute-start | bytes 3145736 | tf_op jit(solution)/shard_map/ppermute | solution.py:10
  262.4 2.1 collective-permute-done.4
  264.5 25.1 %collective-permute-start.5 = (bf16[512,1024]{1,0:T(8,128)(2,1)S(1)}, bf16[512,1024]{1,0:T(8,128)(2,1)S(1)}, u32[]{:S(2)}, u32[]{:S(2)}) collective-permute-start(bf16[512,1024]{1,0:T(8,128)(2,1)S(1)} %broadcast_select_fusion.7), channel_id=1, source_target_pairs={{16,0},{24,8},{32,16},{40,24},{48,32},{56,40},{64,48},{72,56},{80,... | collective-permute-start | bytes 3145736 | tf_op jit(solution)/shard_map/ppermute | solution.py:10
  289.9 24.0 %collective-permute-done.5 = bf16[512,1024]{1,0:T(8,128)(2,1)S(1)} collective-permute-done((bf16[512,1024]{1,0:T(8,128)(2,1)S(1)}, bf16[512,1024]{1,0:T(8,128)(2,1)S(1)}, u32[]{:S(2)}, u32[]{:S(2)}) %collective-permute-start.5) | collective-permute-done | bytes 1048608 | tf_op jit(solution)/shard_map/ppermute | solution.py:10
  314.1 63.0 %collective-permute-done.13 = bf16[512,1024]{1,0:T(8,128)(2,1)S(1)} collective-permute-done((bf16[512,1024]{1,0:T(8,128)(2,1)S(1)}, bf16[512,1024]{1,0:T(8,128)(2,1)S(1)}, u32[]{:S(2)}, u32[]{:S(2)}) %collective-permute-start.13) | collective-permute-done | bytes 1048608 | tf_op jit(solution)/shard_map/ppermute | solution.py:10
  377.3 3.0 collective-permute-start.14
  380.3 112.2 %collective-permute-done.6 = bf16[512,1024]{1,0:T(8,128)(2,1)S(1)} collective-permute-done((bf16[512,1024]{1,0:T(8,128)(2,1)S(1)}, bf16[512,1024]{1,0:T(8,128)(2,1)S(1)}, u32[]{:S(2)}, u32[]{:S(2)}) %collective-permute-start.6) | collective-permute-done | bytes 1048608 | tf_op jit(solution)/shard_map/ppermute | solution.py:10
  493.8 21.3 %collective-permute-done.7 = bf16[512,1024]{1,0:T(8,128)(2,1)S(1)} collective-permute-done((bf16[512,1024]{1,0:T(8,128)(2,1)S(1)}, bf16[512,1024]{1,0:T(8,128)(2,1)S(1)}, u32[]{:S(2)}, u32[]{:S(2)}) %collective-permute-start.7) | collective-permute-done | bytes 1048608 | tf_op jit(solution)/shard_map/ppermute | solution.py:10
  515.1 2.4 convert_add_fusion
  517.5 105.8 %reduce-scatter.2.cloned.1.call-done = f32[512,128]{1,0:T(8,128)} async-done(((f32[512,1024]{1,0:T(8,128)}), f32[512,128]{1,0:T(8,128)}) %reduce-scatter.2.cloned.1.call-update) | async-done | bytes 262160 | tf_op jit(solution)/shard_map/reduce_scatter | solution.py:52
  (34 shorter events, 11.9 us)
Async XLA Ops:
  6.5 616.8 %reduce-scatter.2.cloned.1.call-start = ((), (), s32[]{:S(2)}) async-start(), calls=%async_computation.1 | async-start | bytes 2359296 | tf_op jit(solution)/shard_map/reduce_scatter | solution.py:52
  6.5 15.1 %collective-permute-start = (bf16[512,1024]{1,0:T(8,128)(2,1)}, bf16[512,1024]{1,0:T(8,128)(2,1)S(1)}, u32[]{:S(2)}, u32[]{:S(2)}) collective-permute-start(bf16[512,1024]{1,0:T(8,128)(2,1)} %bitcast.33), channel_id=1, source_target_pairs={{248,0},{0,8},{8,16},{16,24},{24,32},{32,40},{40,48},{48,56},{56,6... | collective-permute-start | bytes 3145736 | tf_op jit(solution)/shard_map/ppermute | solution.py:10
  23.0 23.2 %collective-permute-start.8 = (bf16[512,1024]{1,0:T(8,128)(2,1)S(1)}, bf16[512,1024]{1,0:T(8,128)(2,1)}, u32[]{:S(2)}, u32[]{:S(2)}) collective-permute-start(bf16[512,1024]{1,0:T(8,128)(2,1)S(1)} %get-tuple-element.5), channel_id=1, source_target_pairs={{240,0},{248,8},{0,16},{8,24},{16,32},{24,40},{32,48},{40,56},{48,... | collective-permute-start | bytes 3145736 | tf_op jit(solution)/shard_map/ppermute | solution.py:10
  24.7 43.9 %collective-permute-start.1 = (bf16[512,1024]{1,0:T(8,128)(2,1)S(1)}, bf16[512,1024]{1,0:T(8,128)(2,1)}, u32[]{:S(2)}, u32[]{:S(2)}) collective-permute-start(bf16[512,1024]{1,0:T(8,128)(2,1)S(1)} %get-tuple-element.6), channel_id=1, source_target_pairs={{240,0},{248,8},{0,16},{8,24},{16,32},{24,40},{32,48},{40,56},{48,... | collective-permute-start | bytes 3145736 | tf_op jit(solution)/shard_map/ppermute | solution.py:10
  46.3 65.6 %collective-permute-start.9 = (bf16[512,1024]{1,0:T(8,128)(2,1)S(1)}, bf16[512,1024]{1,0:T(8,128)(2,1)}, u32[]{:S(2)}, u32[]{:S(2)}) collective-permute-start(bf16[512,1024]{1,0:T(8,128)(2,1)S(1)} %broadcast_select_fusion.3), channel_id=1, source_target_pairs={{224,0},{232,8},{240,16},{248,24},{0,32},{8,40},{16,48},{24,56},{3... | collective-permute-start | bytes 3145736 | tf_op jit(solution)/shard_map/ppermute | solution.py:10
  68.7 83.5 %collective-permute-start.2 = (bf16[512,1024]{1,0:T(8,128)(2,1)S(1)}, bf16[512,1024]{1,0:T(8,128)(2,1)}, u32[]{:S(2)}, u32[]{:S(2)}) collective-permute-start(bf16[512,1024]{1,0:T(8,128)(2,1)S(1)} %broadcast_select_fusion.10), channel_id=1, source_target_pairs={{224,0},{232,8},{240,16},{248,24},{0,32},{8,40},{16,48},{24,56},{3... | collective-permute-start | bytes 3145736 | tf_op jit(solution)/shard_map/ppermute | solution.py:10
  112.0 52.8 %copy-start.1 = (f32[32]{0:T(128)S(1)}, f32[32]{0:T(128)}, u32[]{:S(2)}) copy-start(f32[32]{0:T(128)} %param.5) | copy-start | bytes 388
  112.0 76.0 %copy-start.2 = (f32[512]{0:T(512)S(1)}, f32[512]{0:T(512)}, u32[]{:S(2)}) copy-start(f32[512]{0:T(512)} %param.6) | copy-start | bytes 6148
  112.0 76.0 %collective-permute-start.10 = (bf16[512,1024]{1,0:T(8,128)(2,1)S(1)}, bf16[512,1024]{1,0:T(8,128)(2,1)}, u32[]{:S(2)}, u32[]{:S(2)}) collective-permute-start(bf16[512,1024]{1,0:T(8,128)(2,1)S(1)} %broadcast_select_fusion.5), channel_id=1, source_target_pairs={{192,0},{200,8},{208,16},{216,24},{224,32},{232,40},{240,48},{248,... | collective-permute-start | bytes 3145736 | tf_op jit(solution)/shard_map/ppermute | solution.py:10
  153.6 56.4 %collective-permute-start.3 = (bf16[512,1024]{1,0:T(8,128)(2,1)S(1)}, bf16[512,1024]{1,0:T(8,128)(2,1)S(1)}, u32[]{:S(2)}, u32[]{:S(2)}) collective-permute-start(bf16[512,1024]{1,0:T(8,128)(2,1)S(1)} %broadcast_select_fusion.12), channel_id=1, source_target_pairs={{192,0},{200,8},{208,16},{216,24},{224,32},{232,40},{240,48},{248,... | collective-permute-start | bytes 3145736 | tf_op jit(solution)/shard_map/ppermute | solution.py:10
  188.1 3.4 copy-start
  192.2 70.0 %collective-permute-start.11 = (bf16[512,1024]{1,0:T(8,128)(2,1)S(1)}, bf16[512,1024]{1,0:T(8,128)(2,1)S(1)}, u32[]{:S(2)}, u32[]{:S(2)}) collective-permute-start(bf16[512,1024]{1,0:T(8,128)(2,1)S(1)} %convolution_convert_fusion), channel_id=1, source_target_pairs={{8,0},{16,8},{24,16},{32,24},{40,32},{48,40},{56,48},{64,56},{72,6... | collective-permute-start | bytes 3145736 | tf_op jit(solution)/shard_map/ppermute | solution.py:10
  212.8 51.7 %collective-permute-start.4 = (bf16[512,1024]{1,0:T(8,128)(2,1)S(1)}, bf16[512,1024]{1,0:T(8,128)(2,1)S(1)}, u32[]{:S(2)}, u32[]{:S(2)}) collective-permute-start(bf16[512,1024]{1,0:T(8,128)(2,1)S(1)} %convolution_convert_fusion.1), channel_id=1, source_target_pairs={{8,0},{16,8},{24,16},{32,24},{40,32},{48,40},{56,48},{64,56},{72,6... | collective-permute-start | bytes 3145736 | tf_op jit(solution)/shard_map/ppermute | solution.py:10
  262.3 27.4 %collective-permute-start.12 = (bf16[512,1024]{1,0:T(8,128)(2,1)S(1)}, bf16[512,1024]{1,0:T(8,128)(2,1)S(1)}, u32[]{:S(2)}, u32[]{:S(2)}) collective-permute-start(bf16[512,1024]{1,0:T(8,128)(2,1)S(1)} %broadcast_select_fusion), channel_id=1, source_target_pairs={{16,0},{24,8},{32,16},{40,24},{48,32},{56,40},{64,48},{72,56},{80,... | collective-permute-start | bytes 3145736 | tf_op jit(solution)/shard_map/ppermute | solution.py:10
  264.5 49.4 %collective-permute-start.5 = (bf16[512,1024]{1,0:T(8,128)(2,1)S(1)}, bf16[512,1024]{1,0:T(8,128)(2,1)S(1)}, u32[]{:S(2)}, u32[]{:S(2)}) collective-permute-start(bf16[512,1024]{1,0:T(8,128)(2,1)S(1)} %broadcast_select_fusion.7), channel_id=1, source_target_pairs={{16,0},{24,8},{32,16},{40,24},{48,32},{56,40},{64,48},{72,56},{80,... | collective-permute-start | bytes 3145736 | tf_op jit(solution)/shard_map/ppermute | solution.py:10
  289.8 87.3 %collective-permute-start.13 = (bf16[512,1024]{1,0:T(8,128)(2,1)S(1)}, bf16[512,1024]{1,0:T(8,128)(2,1)S(1)}, u32[]{:S(2)}, u32[]{:S(2)}) collective-permute-start(bf16[512,1024]{1,0:T(8,128)(2,1)S(1)} %broadcast_select_fusion.2), channel_id=1, source_target_pairs={{32,0},{40,8},{48,16},{56,24},{64,32},{72,40},{80,48},{88,56},{96,... | collective-permute-start | bytes 3145736 | tf_op jit(solution)/shard_map/ppermute | solution.py:10
  314.0 178.4 %collective-permute-start.6 = (bf16[512,1024]{1,0:T(8,128)(2,1)S(1)}, bf16[512,1024]{1,0:T(8,128)(2,1)S(1)}, u32[]{:S(2)}, u32[]{:S(2)}) collective-permute-start(bf16[512,1024]{1,0:T(8,128)(2,1)S(1)} %broadcast_select_fusion.9), channel_id=1, source_target_pairs={{32,0},{40,8},{48,16},{56,24},{64,32},{72,40},{80,48},{88,56},{96,... | collective-permute-start | bytes 3145736 | tf_op jit(solution)/shard_map/ppermute | solution.py:10
  377.3 116.5 %collective-permute-start.14 = (bf16[512,1024]{1,0:T(8,128)(2,1)S(1)}, bf16[512,1024]{1,0:T(8,128)(2,1)S(1)}, u32[]{:S(2)}, u32[]{:S(2)}) collective-permute-start(bf16[512,1024]{1,0:T(8,128)(2,1)S(1)} %broadcast_select_fusion.4), channel_id=1, source_target_pairs={{64,0},{72,8},{80,16},{88,24},{96,32},{104,40},{112,48},{120,56},{... | collective-permute-start | bytes 3145736 | tf_op jit(solution)/shard_map/ppermute | solution.py:10
  492.6 22.5 %collective-permute-start.7 = (bf16[512,1024]{1,0:T(8,128)(2,1)S(1)}, bf16[512,1024]{1,0:T(8,128)(2,1)S(1)}, u32[]{:S(2)}, u32[]{:S(2)}) collective-permute-start(bf16[512,1024]{1,0:T(8,128)(2,1)S(1)} %broadcast_select_fusion.11), channel_id=1, source_target_pairs={{64,0},{72,8},{80,16},{88,24},{96,32},{104,40},{112,48},{120,56},{... | collective-permute-start | bytes 3145736 | tf_op jit(solution)/shard_map/ppermute | solution.py:10
Sparse Core Ops, SparseCore 0:
  517.6 105.6 reduce-scatter.1
where the time goes:
time: 631 us; the launch traced here: 630 us
  waiting for transfers between devices  464 us (74%)
  starting transfers between devices  131 us (21%)
  between operations  20.2 us (3%)
  matrix products  10 us (2%)
    ppermute x15, waiting for transfers between devices, shifted(): return lax.ppermute(block, axis, route)  358 us
    ppermute x15, starting transfers between devices, shifted(): return lax.ppermute(block, axis, route)  131 us
    reduce_scatter x1, waiting for transfers between devices, per_device(): gamma = lax.psum_scatter(total, 'rep', scatter_dimension=1, tiled=True)  106 us
  transfers between devices with their start and end apart: 16, of which 12 were waited for; matrix products, arithmetic and copies ran while one was open for 2% of the time, Pallas kernels for 0%

commit v1 on v0

v1 whole, which is shorter than its diff:
```python
import functools

import jax
import jax.numpy as jnp
from jax import lax
from jax.experimental import pallas as pl
from jax.experimental.pallas import tpu as pltpu
from jax.sharding import PartitionSpec as P

MESH = pl.DeviceIdType.MESH
F32 = jnp.float32
BF16 = jnp.bfloat16

NZ, NY, NX = 8, 4, 4
ORBS = 32
SIGNS = (1, 2, 2, 2, 1)
BASES = (0, 256, 768, 1280, 1792)
ROWS = (256, 512, 512, 512, 256)
SUB = 32


def row_of(g, par, kind, sgn, q):
    return BASES[g] + ((par * 2 + kind) * SIGNS[g] + sgn) * 64 + SUB * q


def entries_of(g):
    out = []
    for par in range(2):
        for kind in range(2):
            for sgn in range(SIGNS[g]):
                out.append((par, kind, g if sgn else -g))
    return out


class Copies:
    def __init__(self, send_sem, recv_sem):
        self.send_sem, self.recv_sem = send_sem, recv_sem
        self.made = {}

    def start(self, name, src, dst, device):
        n = len(self.made)
        copy = pltpu.make_async_remote_copy(
            src_ref=src, dst_ref=dst, send_sem=self.send_sem.at[n],
            recv_sem=self.recv_sem.at[n], device_id=device, device_id_type=MESH,
        )
        self.made[name] = copy
        copy.start()

    def arrived(self, name):
        self.made[name].wait_recv()

    def finish(self):
        for copy in self.made.values():
            copy.wait_send()


N_COPIES = 96


def kernel(b_ref, ev_ref, eo_ref, off_ref, out_ref, g_ref, inv_ref, ct_ref, w_ref, evc_ref, amp_ref,
           acc_ref, sb_ref, offb_ref, offr_ref, ry_ref, rly_ref, rx_ref, rlx_ref, t2_ref, rl2_ref,
           rx2_ref, t3_ref, rl3_ref, ry2_ref, send_sem, recv_sem, local_sem):
    blk = lax.axis_index("blk")
    rep = lax.axis_index("rep")
    core = lax.rem(blk, 2)
    z = lax.rem(lax.div(blk, 2), NZ)
    x_lo = lax.div(blk, 2 * NZ)
    y = lax.rem(rep, NY)
    x_hi = lax.div(rep, NY)
    x = 2 * x_hi + x_lo

    def device(xx, yy, zz, cc):
        return (lax.rem(xx, 2) * (2 * NZ) + zz * 2 + cc, lax.div(xx, 2) * NY + yy)

    x_r, x_l = lax.rem(x + 1, NX), lax.rem(x + NX - 1, NX)
    y_r, y_l = lax.rem(y + 1, NY), lax.rem(y + NY - 1, NY)
    y_o = lax.rem(y + 2, NY)
    z_r, z_l = lax.rem(z + 1, NZ), lax.rem(z + NZ - 1, NZ)
    zs = (device(x, y, z_r, core), device(x, y, z_l, core))
    xs = (device(x_r, y, z, core), device(x_l, y, z, core))
    ys = (device(x, y_r, z, core), device(x, y_l, z, core))
    sib = device(x, y, z, 1 - core)

    rows8 = lax.broadcasted_iota(jnp.int32, (8, 128), 0)
    offb_ref[0] = jnp.where(rows8 == 0, off_ref[0], jnp.where(rows8 == 1, off_ref[1], -1))

    barrier = pltpu.get_barrier_semaphore()
    for who in (*zs, *xs, *ys, sib):
        pl.semaphore_signal(barrier, inc=1, device_id=who, device_id_type=MESH)
    pl.semaphore_wait(barrier, 7)

    copies = Copies(send_sem, recv_sem)
    mine = pl.multiple_of(128 * y + 64 * x_hi, 64)

    def same(g, sgn, q, count=1):
        if g == 0:
            return b_ref.at[pl.ds(mine + SUB * q, SUB * count), :]
        return g_ref.at[pl.ds(row_of(g, 0, 0, sgn, q), SUB * count), :]

    def slot(g, par, kind, sgn, q, count=1):
        return g_ref.at[pl.ds(row_of(g, par, kind, sgn, q), SUB * count), :]

    def z_send(d, s, q):
        sgn = d if SIGNS[s] == 2 else 0
        to = d if SIGNS[s + 1] == 2 else 0
        copies.start(("z", d, s, q), same(s, sgn, q), slot(s + 1, 0, 0, to, q), zs[d])

    def x_send(g, sgn, q):
        copies.start(("x", g, sgn, q), same(g, sgn, q), slot(g, 0, 1, sgn, q), xs[q])

    def sib_send(g, kind, sgn, q, count=1):
        src = same(g, sgn, q, count) if kind == 0 else slot(g, 0, 1, sgn, q, count)
        copies.start(("s", g, kind, sgn, q), src, slot(g, 1, kind, sgn, q, count), sib)

    for f in range(2):
        z_send(0, 0, f)
        z_send(1, 0, 1 - f)
    for q in range(2):
        x_send(0, 0, q)
    sib_send(0, 0, 0, 0, 2)
    for d in range(2):
        copies.start(("o", d), offb_ref.at[0], offb_ref.at[1 + d], ys[d])
    local = pltpu.make_async_copy(b_ref.at[pl.ds(mine, 64), :], slot(0, 0, 0, 0, 0, 2), local_sem)
    local.start()

    lanes = lax.broadcasted_iota(jnp.int32, (1, 128), 1)
    low = lanes < 64
    ev_y = ev_ref[:, pl.ds(pl.multiple_of(128 * y, 128), 128)]
    ev_swap = jnp.concatenate([ev_y[:, 64:], ev_y[:, :64]], axis=1)
    e_k = eo_ref[blk]
    half_of_lane = lax.div(lanes, 64)
    quarter = lax.rem(lax.div(lanes, SUB), 2)
    half_flip = jnp.where(quarter == 0, lax.div(x_l, 2), lax.div(x_r, 2))
    distances = []
    for g in range(5):
        ents = entries_of(g)
        for n in range(0, len(ents), 2):
            e_l, dist, half = [], [], []
            for par, kind, dz in ents[n:n + 2]:
                c = core if par == 0 else 1 - core
                xl = x_lo if kind == 0 else 1 - x_lo
                orb = xl * (2 * NZ) + lax.rem(z + dz + NZ, NZ) * 2 + c
                gap = lax.rem(blk - orb + ORBS, ORBS)
                e_l.append(eo_ref[orb])
                dist.append(jnp.minimum(gap, ORBS - gap))
                half.append(jnp.full((1, 128), x_hi, jnp.int32) if kind == 0 else half_flip)
            want = jnp.where(low, half[0], half[1])
            ev_b = jnp.where(want == half_of_lane, ev_y, ev_swap)
            col = BASES[g] + 64 * n
            ct_ref[:, col:col + 128] = ev_b - e_k - jnp.where(low, e_l[0], e_l[1])
            distances.append((col, jnp.where(low, dist[0], dist[1])))
    for n in range(4):
        tile = jnp.broadcast_to(ev_ref[:, 128 * n:128 * n + 128], (128, 128))
        evc_ref[128 * n:128 * n + 128, :] = tile.T

    def invert(i, carry):
        rows = pl.ds(pl.multiple_of(i * 32, 32), 32)
        ev_a = evc_ref[rows, :]
        for n in range(16):
            cols = slice(128 * n, 128 * n + 128)
            inv_ref[rows, cols] = -1.0 / (ev_a + ct_ref[:, cols])
        return carry

    lax.fori_loop(0, 16, invert, 0)

    def weigh():
        table = offb_ref[...].reshape(64, 128)
        for col, dist in distances:
            count = jnp.sum(jnp.where(table == dist, 1.0, 0.0), axis=0, keepdims=True)
            w_ref[:, col:col + 128] = jnp.where(dist == 0, 2.0 * count, count)

    def amplitudes(g):
        for n in range(ROWS[g] // 256):
            cols = slice(BASES[g] + 256 * n, BASES[g] + 256 * n + 256)
            right = g_ref[cols, :]
            weight = w_ref[:, cols]
            for m in range(2):
                rows = slice(256 * m, 256 * m + 256)
                pair = lax.dot_general(b_ref[rows, :], right, (((1,), (1,)), ((), ())),
                                       preferred_element_type=F32)
                amp_ref[rows, 256 * n:256 * n + 256] = (pair * (inv_ref[rows, cols] * weight)).astype(BF16)

    def contract(g, rows, final=False):
        for n in range(4):
            res = jnp.dot(amp_ref[rows, :ROWS[g]], g_ref[BASES[g]:BASES[g] + ROWS[g], 256 * n:256 * n + 256],
                          preferred_element_type=F32)
            for h in range(2):
                j = 2 * n + h
                xh, yy = j // NY, j % NY
                val = res[:, 128 * h:128 * h + 128]
                if g > 0:
                    val = val + acc_ref[yy, xh, rows, :]
                acc_ref[yy, xh, rows, :] = val
                if final:
                    sb_ref[yy, xh, rows, :] = val.astype(BF16)

    def group(g):
        for sgn in range(SIGNS[g]):
            if g == 0:
                copies.arrived(("s", 0, 0, 0, 0))
            else:
                for q in range(2):
                    copies.arrived(("s", g, 0, sgn, q))
            for q in range(2):
                copies.arrived(("s", g, 1, sgn, q))
        if g == 0:
            local.wait()
        amplitudes(g)

    def x_arrivals(g):
        for sgn in range(SIGNS[g]):
            for q in range(2):
                copies.arrived(("x", g, sgn, q))
                sib_send(g, 1, sgn, q)

    for s in range(1, 5):
        for f in range(2):
            if s == 4 and f == 1:
                continue
            for d in range(2):
                q = f if d == 0 else 1 - f
                copies.arrived(("z", d, s - 1, q))
                sgn = d if SIGNS[s] == 2 else 0
                if s < 3 or (s == 3 and f == 0):
                    z_send(d, s, q)
                x_send(s, sgn, q)
                sib_send(s, 0, sgn, q)
            if f == 0:
                x_arrivals(s - 1)
                if s == 1:
                    copies.arrived(("o", 0))
                    copies.start(("o", 2), offb_ref.at[1], offb_ref.at[3], ys[0])
                if s == 2:
                    copies.arrived(("ox", 0))
                    copies.start(("ox", 1), offr_ref, offb_ref.at[pl.ds(4, 4)], xs[0])
            if f == 1 and s == 1:
                copies.arrived(("o", 1))
                copies.arrived(("o", 2))
                copies.start(("ox", 0), offb_ref.at[pl.ds(0, 4)], offr_ref, xs[0])
        if s == 3:
            copies.arrived(("ox", 1))
            weigh()
            for g in range(2):
                group(g)
                contract(g, slice(0, 512))
        if s == 4:
            group(2)
            contract(2, slice(0, 512))
            group(3)
            contract(3, slice(0, 512))
    x_arrivals(4)
    group(4)

    lo, hi = slice(0, 256), slice(256, 512)
    other = 1 - x_hi
    contract(4, hi, True)
    for d in range(2):
        copies.start(("x1", d), sb_ref.at[pl.ds(2 * d, 2), other, pl.ds(256, 256), :], rlx_ref.at[d], xs[d])
    contract(4, lo, True)
    for d, to in enumerate((y_r, y_l)):
        copies.start(("y1r", d), sb_ref.at[y_o, d, pl.ds(0, 256), :], rly_ref.at[d], ys[d])
        copies.start(("y1", d), sb_ref.at[to, :, pl.ds(0, 256), :], ry_ref.at[d], ys[d])
    for d in range(2):
        copies.arrived(("x1", d))
        copies.start(("x1f", d), rlx_ref.at[d], rx_ref.at[pl.ds(2 * d, 2)], xs[d])
    for d in range(2):
        copies.arrived(("y1r", d))
        copies.start(("y1f", d), rly_ref.at[d], ry_ref.at[2, d], ys[d])
    for d in range(2):
        copies.arrived(("x1f", d))
    for yy in range(NY):
        t3_ref[yy] = (acc_ref[yy, x_hi, hi, :] + rx_ref[yy].astype(F32)).astype(BF16)
    for d, to in enumerate((y_r, y_l)):
        copies.start(("y2r", d), t3_ref.at[y_o, pl.ds(128 * d, 128), :], rl3_ref.at[d], ys[d])
        copies.start(("y2", d), t3_ref.at[to], ry2_ref.at[d], ys[d])
    for d in range(2):
        copies.arrived(("y1", d))
    for d in range(2):
        copies.arrived(("y1f", d))

    def y_sum(which):
        return (acc_ref[y, which, lo, :] + ry_ref[0, which].astype(F32) + ry_ref[1, which].astype(F32)
                + ry_ref[2, which].astype(F32))

    t2_ref[...] = y_sum(other).astype(BF16)
    for d in range(2):
        copies.start(("x2", d), t2_ref.at[pl.ds(128 * d, 128), :], rl2_ref.at[d], xs[d])
    for d in range(2):
        copies.arrived(("y2r", d))
        copies.start(("y2f", d), rl3_ref.at[d], ry2_ref.at[2, pl.ds(128 * d, 128), :], ys[d])
    for d in range(2):
        copies.arrived(("x2", d))
        copies.start(("x2f", d), rl2_ref.at[d], rx2_ref.at[pl.ds(128 * d, 128), :], xs[d])
    for d in range(2):
        copies.arrived(("y2", d))
    for d in range(2):
        copies.arrived(("y2f", d))
    out_ref[0, hi, :] = (acc_ref[y, x_hi, hi, :] + rx_ref[y].astype(F32) + ry2_ref[0].astype(F32)
                         + ry2_ref[1].astype(F32) + ry2_ref[2].astype(F32))
    for d in range(2):
        copies.arrived(("x2f", d))
    out_ref[0, lo, :] = y_sum(x_hi) + rx2_ref[...].astype(F32)
    copies.finish()


def per_device(integrals, eps_occ, eps_vir, offsets):
    v, aux = integrals.shape[1:]
    vmem = pl.BlockSpec(memory_space=pltpu.VMEM)
    smem = pl.BlockSpec(memory_space=pltpu.SMEM)
    return pl.pallas_call(
        kernel,
        out_shape=jax.ShapeDtypeStruct((1, v, aux // 8), F32),
        in_specs=[vmem, vmem, smem, smem],
        out_specs=vmem,
        scratch_shapes=[
            pltpu.VMEM((2048, aux), BF16),
            pltpu.VMEM((v, 2048), F32),
            pltpu.VMEM((1, 2048), F32),
            pltpu.VMEM((1, 2048), F32),
            pltpu.VMEM((v, 128), F32),
            pltpu.VMEM((v, 512), BF16),
            pltpu.VMEM((NY, 2, v, 128), F32),
            pltpu.VMEM((NY, 2, v, 128), BF16),
            pltpu.VMEM((8, 8, 128), jnp.int32),
            pltpu.VMEM((4, 8, 128), jnp.int32),
            pltpu.VMEM((3, 2, 256, 128), BF16),
            pltpu.VMEM((2, 256, 128), BF16),
            pltpu.VMEM((4, 256, 128), BF16),
            pltpu.VMEM((2, 2, 256, 128), BF16),
            pltpu.VMEM((256, 128), BF16),
            pltpu.VMEM((2, 128, 128), BF16),
            pltpu.VMEM((256, 128), BF16),
            pltpu.VMEM((NY, 256, 128), BF16),
            pltpu.VMEM((2, 128, 128), BF16),
            pltpu.VMEM((3, 256, 128), BF16),
            pltpu.SemaphoreType.DMA((N_COPIES,)),
            pltpu.SemaphoreType.DMA((N_COPIES,)),
            pltpu.SemaphoreType.DMA,
        ],
        compiler_params=pltpu.CompilerParams(
            collective_id=0, has_side_effects=True, vmem_limit_bytes=56 << 20
        ),
        name="pair_amplitudes",
    )(integrals[0], eps_vir[None, :], eps_occ, offsets)


def solution(mesh):
    in_specs = (P("blk", None, None), P(), P(), P("rep"))
    out_specs = P("blk", None, "rep")
    return jax.shard_map(
        per_device, mesh=mesh, in_specs=in_specs, out_specs=out_specs, check_vma=False
    )
```

time: 631 us -> 53.4 us (0.08)
  the two profiles are of different devices: /device:TPU:1 before, /device:TPU:2 now
where the time goes in v1:
time: 53.4 us; the launch traced here: 53.3 us
  Pallas kernels  51.6 us (97%)
  local copies, waits for them, and re-layouts  1.67 us (3%)
    pallas_call x1, Pallas kernels, per_device(): pl.pallas_call(kernel, out_shape=jax.ShapeDtypeStruct((1, v, aux // 8), F...  51.6 us
    unnamed x1, local copies, waits for them, and re-layouts  1.67 us

profile of v1, /device:TPU:2, one launch (start us, length us, event | category | flops | bytes accessed | tf_op | source)
XLA Modules:
  0.0 53.3 jit_solution(9770983649196260172)
XLA Ops:
  0.0 51.6 %pair_amplitudes.1 = f32[1,512,128]{2,1,0:T(8,128)} custom-call(bf16[512,1024]{1,0:T(8,128)(2,1)} %bitcast.2, f32[1,512]{1,0:T(1,128)} %bitcast.3, f32[32]{0:T(128)} %eo_ref.1, s32[2]{0:T(128)} %off_ref.1), custom_call_target="tpu_custom_call" | custom-call | tf_op jit(solution)/shard_map/pair_amplitudes/pallas_call | solution.py:310
  51.6 1.7 %copy.6 = f32[1,512,128]{2,1,0:T(8,128)} copy(f32[1,512,128]{2,1,0:T(8,128)} %pair_amplitudes.1) | data formatting | bytes 524288

commit v2 on v0

v2 whole, which is shorter than its diff:
```python
import jax
import jax.numpy as jnp
from jax import lax
from jax.experimental import pallas as pl
from jax.experimental.pallas import tpu as pltpu
from jax.sharding import PartitionSpec as P

MESH = pl.DeviceIdType.MESH
F32 = jnp.float32
BF16 = jnp.bfloat16

NZ, NY, NX = 8, 4, 4
ORBS = 32
PIECE = 16
BLOCK = 256


def row_of(g, par, kind, sgn, c):
    if g in (0, 4):
        entry = (0 if g == 0 else 28) + kind * 2 + par
    else:
        entry = 4 + (g - 1) * 8 + kind * 4 + par * 2 + sgn
    return entry * 64 + PIECE * c


def entry_list():
    out = [None] * 32
    for g in range(5):
        for par in range(2):
            for kind in range(2):
                for sgn in range(1 if g in (0, 4) else 2):
                    out[row_of(g, par, kind, sgn, 0) // 64] = (par, kind, g if sgn else -g)
    return out


class Copies:
    def __init__(self, send_sem, recv_sem):
        self.send_sem, self.recv_sem = send_sem, recv_sem
        self.made = {}

    def start(self, name, src, dst, device):
        n = len(self.made)
        copy = pltpu.make_async_remote_copy(
            src_ref=src, dst_ref=dst, send_sem=self.send_sem.at[n],
            recv_sem=self.recv_sem.at[n], device_id=device, device_id_type=MESH,
        )
        self.made[name] = copy
        copy.start()

    def arrived(self, name):
        self.made[name].wait_recv()

    def finish(self):
        for copy in self.made.values():
            copy.wait_send()


N_COPIES = 176


def kernel(b_ref, ev_ref, eo_ref, off_ref, out_ref, g_ref, inv_ref, ct_ref, w_ref, evc_ref, amp_ref,
           acc_ref, sb_ref, offb_ref, ry_ref, send_sem, recv_sem, local_sem):
    blk = lax.axis_index("blk")
    rep = lax.axis_index("rep")
    core = lax.rem(blk, 2)
    z = lax.rem(lax.div(blk, 2), NZ)
    x_lo = lax.div(blk, 2 * NZ)
    y = lax.rem(rep, NY)
    x_hi = lax.div(rep, NY)
    x = 2 * x_hi + x_lo
    other = 1 - x_hi

    def device(xx, zz, cc):
        return (lax.rem(xx, 2) * (2 * NZ) + zz * 2 + cc, lax.div(xx, 2) * NY + y)

    x_r, x_l = lax.rem(x + 1, NX), lax.rem(x + NX - 1, NX)
    z_r, z_l = lax.rem(z + 1, NZ), lax.rem(z + NZ - 1, NZ)
    zs = (device(x, z_r, core), device(x, z_l, core))
    xs = (device(x_r, z, core), device(x_l, z, core))
    diagonal = (device(x_r, z_r, core), device(x_l, z_l, core))
    sib = device(x, z, 1 - core)
    peers = []
    for dx in (1, 0):
        for dy in (2, 1, 3, 0):
            if dx or dy:
                to = lax.rem(y + dy, NY)
                xh = other if dx else x_hi
                peers.append((blk, xh * NY + to))

    rows8 = lax.broadcasted_iota(jnp.int32, (8, 128), 0)
    offb_ref[7] = jnp.where(rows8 == 0, off_ref[0], jnp.where(rows8 == 1, off_ref[1], -1))

    barrier = pltpu.get_barrier_semaphore()
    greeted = (*zs, *xs, *diagonal, sib, *peers)
    for who in greeted:
        pl.semaphore_signal(barrier, inc=1, device_id=who, device_id_type=MESH)
    pl.semaphore_wait(barrier, len(greeted))

    copies = Copies(send_sem, recv_sem)
    mine = pl.multiple_of(128 * y + 64 * x_hi, 64)

    def slot(g, par, kind, sgn, c, count=1):
        return g_ref.at[pl.ds(row_of(g, par, kind, sgn, c), PIECE * count), :]

    def same(g, sgn, c, count=1):
        if g == 0:
            return b_ref.at[pl.ds(mine + PIECE * c, PIECE * count), :]
        return slot(g, 0, 0, sgn, c, count)

    def sign(g, d):
        return 0 if g in (0, 4) else d

    def z_send(d, s, c):
        copies.start(("z", d, s, c), same(s, sign(s, d), c), slot(s + 1, 0, 0, sign(s + 1, d), c), zs[d])

    def x_send(g, sgn, c, count=1):
        copies.start(("x", g, sgn, c), same(g, sgn, c, count), slot(g, 0, 1, sgn, c, count), xs[c // 2])

    def sib_send(g, kind, sgn, c, count=1):
        src = same(g, sgn, c, count) if kind == 0 else slot(g, 0, 1, sgn, c, count)
        copies.start(("s", g, kind, sgn, c), src, slot(g, 1, kind, sgn, c, count), sib)

    for i in range(4):
        z_send(0, 0, i)
        z_send(1, 0, 3 - i)
        if i == 0:
            for n, who in enumerate(peers):
                copies.start(("o", n), offb_ref.at[7], offb_ref.at[n], who)
    for c in (0, 2):
        x_send(0, 0, c, 2)
    sib_send(0, 0, 0, 0, 4)
    local = pltpu.make_async_copy(b_ref.at[pl.ds(mine, 64), :], slot(0, 0, 0, 0, 0, 4), local_sem)
    local.start()

    lanes = lax.broadcasted_iota(jnp.int32, (1, 128), 1)
    low = lanes < 64
    ev_y = ev_ref[:, pl.ds(pl.multiple_of(128 * y, 128), 128)]
    ev_swap = jnp.concatenate([ev_y[:, 64:], ev_y[:, :64]], axis=1)
    e_k = eo_ref[blk]
    half_of_lane = lax.div(lanes, 64)
    quarter = lax.rem(lax.div(lanes, 32), 2)
    half_flip = jnp.where(quarter == 0, lax.div(x_l, 2), lax.div(x_r, 2))
    distances = []
    ents = entry_list()
    for n in range(0, 32, 2):
        e_l, dist, half = [], [], []
        for par, kind, dz in ents[n:n + 2]:
            c = core if par == 0 else 1 - core
            xl = x_lo if kind == 0 else 1 - x_lo
            orb = xl * (2 * NZ) + lax.rem(z + dz + NZ, NZ) * 2 + c
            gap = lax.rem(blk - orb + ORBS, ORBS)
            e_l.append(eo_ref[orb])
            dist.append(jnp.minimum(gap, ORBS - gap))
            half.append(jnp.full((1, 128), x_hi, jnp.int32) if kind == 0 else half_flip)
        want = jnp.where(low, half[0], half[1])
        ev_b = jnp.where(want == half_of_lane, ev_y, ev_swap)
        ct_ref[:, 64 * n:64 * n + 128] = ev_b - e_k - jnp.where(low, e_l[0], e_l[1])
        distances.append((64 * n, jnp.where(low, dist[0], dist[1])))
    for n in range(4):
        tile = jnp.broadcast_to(ev_ref[:, 128 * n:128 * n + 128], (128, 128))
        evc_ref[128 * n:128 * n + 128, :] = tile.T

    def invert(i, carry):
        rows = pl.ds(pl.multiple_of(i * 32, 32), 32)
        ev_a = evc_ref[rows, :]
        for n in range(16):
            cols = slice(128 * n, 128 * n + 128)
            inv_ref[rows, cols] = -1.0 / (ev_a + ct_ref[:, cols])
        return carry

    lax.fori_loop(0, 16, invert, 0)

    def weigh():
        for n in range(7):
            copies.arrived(("o", n))
        table = offb_ref[...].reshape(64, 128)
        for col, dist in distances:
            count = jnp.sum(jnp.where(table == dist, 1.0, 0.0), axis=0, keepdims=True)
            w_ref[:, col:col + 128] = jnp.where(dist == 0, 2.0 * count, count)

    def amplitudes(n):
        cols = slice(BLOCK * n, BLOCK * n + BLOCK)
        right = g_ref[cols, :]
        weight = w_ref[:, cols]
        for m in range(2):
            rows = slice(256 * m, 256 * m + 256)
            pair = lax.dot_general(b_ref[rows, :], right, (((1,), (1,)), ((), ())),
                                   preferred_element_type=F32)
            amp_ref[n % 2, rows, :] = (pair * (inv_ref[rows, cols] * weight)).astype(BF16)

    def contract(n):
        for m in range(4):
            res = jnp.dot(amp_ref[n % 2], g_ref[BLOCK * n:BLOCK * n + BLOCK, 256 * m:256 * m + 256],
                          preferred_element_type=F32)
            for h in range(2):
                val = res[:, 128 * h:128 * h + 128]
                if n > 0:
                    val = val + acc_ref[2 * m + h]
                acc_ref[2 * m + h] = val

    def contract_last(which, rows):
        for m in range(2):
            cols = pl.ds(pl.multiple_of(which * 512 + 256 * m, 256), 256)
            res = jnp.dot(amp_ref[1, rows, :], g_ref[7 * BLOCK:, cols], preferred_element_type=F32)
            for h in range(2):
                j = which * NY + 2 * m + h
                val = res[:, 128 * h:128 * h + 128] + acc_ref[j, rows, :]
                acc_ref[j, rows, :] = val
                sb_ref[j, rows, :] = val.astype(BF16)

    def sib_arrived(g, kind):
        for sgn in range(1 if g in (0, 4) else 2):
            if g == 0 and kind == 0:
                copies.arrived(("s", 0, 0, 0, 0))
            elif g == 4:
                for c in range(4):
                    copies.arrived(("s", g, kind, 0, c))
            else:
                for c in (0, 2):
                    copies.arrived(("s", g, kind, sgn, c))

    def x_arrivals(g, i):
        if g == 0:
            for c in (0, 2):
                copies.arrived(("x", 0, 0, c))
                sib_send(0, 1, 0, c, 2)
            return
        for d, c in ((0, i), (1, 3 - i)):
            copies.arrived(("x", g, d, c))
            if i % 2 == 1:
                sib_send(g, 1, d, c // 2 * 2, 2)

    for s in range(1, 5):
        for i in range(4 if s < 4 else 2):
            for d, c in ((0, i), (1, 3 - i)):
                copies.arrived(("z", d, s - 1, c))
                if s < 3 or (s == 3 and i < 2):
                    z_send(d, s, c)
                if s == 3 and i < 2:
                    copies.start(("d", d, c), slot(3, 0, 0, d, c), slot(4, 0, 1, 0, c), diagonal[d])
            for d, c in ((0, i), (1, 3 - i)):
                if s < 4:
                    x_send(s, d, c)
                    if i % 2 == 1:
                        sib_send(s, 0, d, c // 2 * 2, 2)
                else:
                    sib_send(4, 0, 0, c)
            if s == 1 and i == 1:
                x_arrivals(0, 0)
            if s > 1:
                if i > 0:
                    x_arrivals(s - 1, i - 1)
            if i == 3 and s > 1:
                x_arrivals(s - 1, 3)
            if (s, i) == (1, 3):
                weigh()
                sib_arrived(0, 0)
                sib_arrived(0, 1)
                local.wait()
                amplitudes(0)
                contract(0)
            if (s, i) == (2, 1):
                sib_arrived(1, 0)
                amplitudes(1)
            if (s, i) == (2, 2):
                contract(1)
            if (s, i) == (3, 1):
                sib_arrived(1, 1)
                amplitudes(2)
            if (s, i) == (3, 2):
                contract(2)
                sib_arrived(2, 0)
                amplitudes(3)
            if (s, i) == (3, 3):
                contract(3)
            if (s, i) == (4, 0):
                sib_arrived(2, 1)
                amplitudes(4)
            if (s, i) == (4, 1):
                for d, c in ((0, 0), (1, 3), (0, 1), (1, 2)):
                    copies.arrived(("d", d, c))
                    sib_send(4, 1, 0, c)
                for j in (1, 2, 3):
                    x_arrivals(3, j)
                contract(4)
                sib_arrived(3, 0)
                amplitudes(5)
                contract(5)
    sib_arrived(3, 1)
    amplitudes(6)
    contract(6)
    sib_arrived(4, 0)
    sib_arrived(4, 1)
    amplitudes(7)

    halves = (slice(0, 256), slice(256, 512))
    for k, which in enumerate((other, x_hi)):
        for m, rows in enumerate(halves):
            contract_last(which, rows)
            for n, who in enumerate(peers):
                if (n < 4) == (k == 0):
                    part = pl.ds(256 * m, 256)
                    copies.start(("r", n, m), sb_ref.at[who[1], part, :], ry_ref.at[n, part, :], who)
    for m, rows in enumerate(halves):
        total = acc_ref[rep, rows, :]
        for n in range(7):
            copies.arrived(("r", n, m))
            total = total + ry_ref[n, rows, :].astype(F32)
        out_ref[0, rows, :] = total
    copies.finish()


def per_device(integrals, eps_occ, eps_vir, offsets):
    v, aux = integrals.shape[1:]
    vmem = pl.BlockSpec(memory_space=pltpu.VMEM)
    smem = pl.BlockSpec(memory_space=pltpu.SMEM)
    return pl.pallas_call(
        kernel,
        out_shape=jax.ShapeDtypeStruct((1, v, aux // 8), F32),
        in_specs=[vmem, vmem, smem, smem],
        out_specs=vmem,
        scratch_shapes=[
            pltpu.VMEM((2048, aux), BF16),
            pltpu.VMEM((v, 2048), F32),
            pltpu.VMEM((1, 2048), F32),
            pltpu.VMEM((1, 2048), F32),
            pltpu.VMEM((v, 128), F32),
            pltpu.VMEM((2, v, BLOCK), BF16),
            pltpu.VMEM((8, v, 128), F32),
            pltpu.VMEM((8, v, 128), BF16),
            pltpu.VMEM((8, 8, 128), jnp.int32),
            pltpu.VMEM((7, v, 128), BF16),
            pltpu.SemaphoreType.DMA((N_COPIES,)),
            pltpu.SemaphoreType.DMA((N_COPIES,)),
            pltpu.SemaphoreType.DMA,
        ],
        compiler_params=pltpu.CompilerParams(
            collective_id=0, has_side_effects=True, vmem_limit_bytes=56 << 20
        ),
        name="pair_amplitudes",
    )(integrals[0], eps_vir[None, :], eps_occ, offsets)


def solution(mesh):
    in_specs = (P("blk", None, None), P(), P(), P("rep"))
    out_specs = P("blk", None, "rep")
    return jax.shard_map(
        per_device, mesh=mesh, in_specs=in_specs, out_specs=out_specs, check_vma=False
    )
```

time: 631 us -> 50.5 us (0.08)
  waiting for transfers between devices: 464 us -> 0 us
  starting transfers between devices: 131 us -> 0 us
  Pallas kernels: 0 us -> 48.7 us
  between operations: 20.2 us -> 0.01 us
  matrix products: 10 us -> 0 us
    ppermute x15 -> x0, waiting for transfers between devices: 358 us -> none  [shifted(): return lax.ppermute(block, axis, route)]
    ppermute x15 -> x0, starting transfers between devices: 131 us -> none  [shifted(): return lax.ppermute(block, axis, route)]
    reduce_scatter x1 -> x0, waiting for transfers between devices: 106 us -> none  [per_device(): gamma = lax.psum_scatter(total, 'rep', scatter_dimension=1, tiled=True)]
    pallas_call x0 -> x1, Pallas kernels: none -> 48.7 us  [per_device(): pl.pallas_call(kernel, out_shape=jax.ShapeDtypeStruct((1, v, aux // 8), F...]
    dot_general x6 -> x0, matrix products: 10 us -> none  [the longest x2 5.41 us: pair_amp(): lax.dot_general(left, right, (((1,), (1,)), ((), ())), preferred_element_...]
  transfers between devices with their start and end apart: 16 -> 0, of which waited for: 12 -> 0; matrix products, arithmetic and copies ran while one was open for 2% -> 0% of each run, Pallas kernels for 0% -> 0%
where the time goes in v2:
time: 50.5 us; the launch traced here: 50.4 us
  Pallas kernels  48.7 us (96%)
  local copies, waits for them, and re-layouts  1.67 us (3%)
    pallas_call x1, Pallas kernels, per_device(): pl.pallas_call(kernel, out_shape=jax.ShapeDtypeStruct((1, v, aux // 8), F...  48.7 us
    unnamed x1, local copies, waits for them, and re-layouts  1.67 us

profile of v2, /device:TPU:1, one launch (start us, length us, event | category | flops | bytes accessed | tf_op | source)
XLA Modules:
  0.0 50.4 jit_solution(16933401985615630469)
XLA Ops:
  0.0 48.7 %pair_amplitudes.1 = f32[1,512,128]{2,1,0:T(8,128)} custom-call(bf16[512,1024]{1,0:T(8,128)(2,1)} %bitcast.2, f32[1,512]{1,0:T(1,128)} %bitcast.3, f32[32]{0:T(128)} %eo_ref.1, s32[2]{0:T(128)} %off_ref.1), custom_call_target="tpu_custom_call" | custom-call | tf_op jit(solution)/shard_map/pair_amplitudes/pallas_call | solution.py:317
  48.7 1.7 %copy.6 = f32[1,512,128]{2,1,0:T(8,128)} copy(f32[1,512,128]{2,1,0:T(8,128)} %pair_amplitudes.1) | data formatting | bytes 524288

commit v3 on v2

--- a/solution.py
+++ b/solution.py
@@ -13,6 +13,7 @@
 ORBS = 32
 PIECE = 16
 BLOCK = 256
+X_FIRST, Y_FIRST, DIRECT = slice(0, 192), slice(192, 384), slice(384, 512)
 
 
 def row_of(g, par, kind, sgn, c):
@@ -59,7 +60,7 @@
 
 
 def kernel(b_ref, ev_ref, eo_ref, off_ref, out_ref, g_ref, inv_ref, ct_ref, w_ref, evc_ref, amp_ref,
-           acc_ref, sb_ref, offb_ref, ry_ref, send_sem, recv_sem, local_sem):
+           acc_ref, sb_ref, offb_ref, rd_ref, rx_ref, ry_ref, t3_ref, ry2_ref, t2_ref, rx2_ref, send_sem, recv_sem, local_sem):
     blk = lax.axis_index("blk")
     rep = lax.axis_index("rep")
     core = lax.rem(blk, 2)
@@ -79,6 +80,9 @@
     xs = (device(x_r, z, core), device(x_l, z, core))
     diagonal = (device(x_r, z_r, core), device(x_l, z_l, core))
     sib = device(x, z, 1 - core)
+    y_r, y_l, y_o = lax.rem(y + 1, NY), lax.rem(y + NY - 1, NY), lax.rem(y + 2, NY)
+    ys = ((blk, x_hi * NY + y_r), (blk, x_hi * NY + y_l), (blk, x_hi * NY + y_o))
+    partner = (blk, other * NY + y)
     peers = []
     for dx in (1, 0):
         for dy in (2, 1, 3, 0):
@@ -88,10 +92,10 @@
                 peers.append((blk, xh * NY + to))
 
     rows8 = lax.broadcasted_iota(jnp.int32, (8, 128), 0)
-    offb_ref[7] = jnp.where(rows8 == 0, off_ref[0], jnp.where(rows8 == 1, off_ref[1], -1))
+    offb_ref[0] = jnp.where(rows8 == 0, off_ref[0], jnp.where(rows8 == 1, off_ref[1], -1))
 
     barrier = pltpu.get_barrier_semaphore()
-    greeted = (*zs, *xs, *diagonal, sib, *peers)
+    greeted = (*zs, *xs, *ys[:2], sib)
     for who in greeted:
         pl.semaphore_signal(barrier, inc=1, device_id=who, device_id_type=MESH)
     pl.semaphore_wait(barrier, len(greeted))
@@ -124,8 +128,8 @@
         z_send(0, 0, i)
         z_send(1, 0, 3 - i)
         if i == 0:
-            for n, who in enumerate(peers):
-                copies.start(("o", n), offb_ref.at[7], offb_ref.at[n], who)
+            for n in range(2):
+                copies.start(("o", n), offb_ref.at[0], offb_ref.at[1 + n], ys[n])
     for c in (0, 2):
         x_send(0, 0, c, 2)
     sib_send(0, 0, 0, 0, 4)
@@ -171,8 +175,7 @@
     lax.fori_loop(0, 16, invert, 0)
 
     def weigh():
-        for n in range(7):
-            copies.arrived(("o", n))
+        copies.arrived(("o", 3))
         table = offb_ref[...].reshape(64, 128)
         for col, dist in distances:
             count = jnp.sum(jnp.where(table == dist, 1.0, 0.0), axis=0, keepdims=True)
@@ -252,23 +255,30 @@
                     x_arrivals(s - 1, i - 1)
             if i == 3 and s > 1:
                 x_arrivals(s - 1, 3)
-            if (s, i) == (1, 3):
-                weigh()
+            if (s, i) == (1, 0):
+                copies.arrived(("o", 0))
+                copies.start(("o", 2), offb_ref.at[1], offb_ref.at[3], ys[0])
+            if (s, i) == (2, 0):
+                copies.arrived(("o", 1))
+                copies.arrived(("o", 2))
+                copies.start(("o", 3), offb_ref.at[pl.ds(0, 4)], offb_ref.at[pl.ds(4, 4)], partner)
+            if (s, i) == (2, 2):
                 sib_arrived(0, 0)
                 sib_arrived(0, 1)
                 local.wait()
+                weigh()
                 amplitudes(0)
                 contract(0)
-            if (s, i) == (2, 1):
+            if (s, i) == (2, 3):
                 sib_arrived(1, 0)
                 amplitudes(1)
-            if (s, i) == (2, 2):
+            if (s, i) == (3, 0):
                 contract(1)
             if (s, i) == (3, 1):
                 sib_arrived(1, 1)
                 amplitudes(2)
+                contract(2)
             if (s, i) == (3, 2):
-                contract(2)
                 sib_arrived(2, 0)
                 amplitudes(3)
             if (s, i) == (3, 3):
@@ -293,25 +303,57 @@
     sib_arrived(4, 1)
     amplitudes(7)
 
-    halves = (slice(0, 256), slice(256, 512))
-    for k, which in enumerate((other, x_hi)):
-        for m, rows in enumerate(halves):
-            contract_last(which, rows)
-            for n, who in enumerate(peers):
-                if (n < 4) == (k == 0):
-                    part = pl.ds(256 * m, 256)
-                    copies.start(("r", n, m), sb_ref.at[who[1], part, :], ry_ref.at[n, part, :], who)
-    for m, rows in enumerate(halves):
-        total = acc_ref[rep, rows, :]
-        for n in range(7):
-            copies.arrived(("r", n, m))
-            total = total + ry_ref[n, rows, :].astype(F32)
-        out_ref[0, rows, :] = total
+    def sliced(ref, which, to, rows):
+        return ref.at[which * NY + to, pl.ds(rows.start, rows.stop - rows.start), :]
+
+    contract_last(other, X_FIRST)
+    copies.start(("x1", 0), sb_ref.at[pl.ds(other * NY, NY), pl.ds(0, 192), :], rx_ref, partner)
+    for which in (0, 1):
+        contract_last(which, Y_FIRST)
+        for n, to in enumerate((y_r, y_l, y_o)):
+            copies.start(("y1", n, which), sliced(sb_ref, which, to, Y_FIRST), ry_ref.at[n, which], ys[n])
+    for which in (0, 1):
+        contract_last(which, DIRECT)
+    for n, who in enumerate(peers):
+        copies.start(("r", n), sb_ref.at[who[1], pl.ds(384, 128), :], rd_ref.at[n], who)
+    contract_last(x_hi, X_FIRST)
+
+    copies.arrived(("x1", 0))
+    for to in range(NY):
+        t3_ref[to] = (acc_ref[x_hi * NY + to, X_FIRST, :] + rx_ref[to].astype(F32)).astype(BF16)
+    for n, to in enumerate((y_r, y_l, y_o)):
+        copies.start(("y2", n), t3_ref.at[to], ry2_ref.at[n], ys[n])
+
+    def y_sum(which):
+        total = acc_ref[which * NY + y, Y_FIRST, :]
+        for n in range(3):
+            total = total + ry_ref[n, which].astype(F32)
+        return total
+
+    for n in range(3):
+        for which in (0, 1):
+            copies.arrived(("y1", n, which))
+    t2_ref[...] = y_sum(other).astype(BF16)
+    copies.start(("x2", 0), t2_ref, rx2_ref, partner)
+    total = acc_ref[rep, DIRECT, :]
+    for n in range(7):
+        copies.arrived(("r", n))
+        total = total + rd_ref[n].astype(F32)
+    out_ref[0, DIRECT, :] = total
+    total = acc_ref[rep, X_FIRST, :] + rx_ref[y].astype(F32)
+    for n in range(3):
+        copies.arrived(("y2", n))
+        total = total + ry2_ref[n].astype(F32)
+    out_ref[0, X_FIRST, :] = total
+    total = y_sum(x_hi)
+    copies.arrived(("x2", 0))
+    out_ref[0, Y_FIRST, :] = total + rx2_ref[...].astype(F32)
     copies.finish()
 
 
 def per_device(integrals, eps_occ, eps_vir, offsets):
     v, aux = integrals.shape[1:]
+    n_x, n_y, n_d = (part.stop - part.start for part in (X_FIRST, Y_FIRST, DIRECT))
     vmem = pl.BlockSpec(memory_space=pltpu.VMEM)
     smem = pl.BlockSpec(memory_space=pltpu.SMEM)
     return pl.pallas_call(
@@ -329,7 +371,13 @@
             pltpu.VMEM((8, v, 128), F32),
             pltpu.VMEM((8, v, 128), BF16),
             pltpu.VMEM((8, 8, 128), jnp.int32),
-            pltpu.VMEM((7, v, 128), BF16),
+            pltpu.VMEM((7, n_d, 128), BF16),
+            pltpu.VMEM((NY, n_x, 128), BF16),
+            pltpu.VMEM((3, 2, n_y, 128), BF16),
+            pltpu.VMEM((NY, n_x, 128), BF16),
+            pltpu.VMEM((3, n_x, 128), BF16),
+            pltpu.VMEM((n_y, 128), BF16),
+            pltpu.VMEM((n_y, 128), BF16),
             pltpu.SemaphoreType.DMA((N_COPIES,)),
             pltpu.SemaphoreType.DMA((N_COPIES,)),
             pltpu.SemaphoreType.DMA,

time: 50.5 us -> 49.3 us (0.976)
  Pallas kernels: 48.7 us -> 47.5 us
    pallas_call x1, Pallas kernels: 48.7 us -> 47.5 us  [per_device(): pl.pallas_call(kernel, out_shape=jax.ShapeDtypeStruct((1, v, aux // 8), F...]
where the time goes in v3:
time: 49.3 us; the launch traced here: 49.1 us
  Pallas kernels  47.5 us (96%)
  local copies, waits for them, and re-layouts  1.67 us (3%)
    pallas_call x1, Pallas kernels, per_device(): pl.pallas_call(kernel, out_shape=jax.ShapeDtypeStruct((1, v, aux // 8), F...  47.5 us
    unnamed x1, local copies, waits for them, and re-layouts  1.67 us

profile of v3, /device:TPU:1, one launch (start us, length us, event | category | flops | bytes accessed | tf_op | source)
XLA Modules:
  0.0 49.1 jit_solution(12155171753371983701)
XLA Ops:
  0.0 47.5 %pair_amplitudes.1 = f32[1,512,128]{2,1,0:T(8,128)} custom-call(bf16[512,1024]{1,0:T(8,128)(2,1)} %bitcast.2, f32[1,512]{1,0:T(1,128)} %bitcast.3, f32[32]{0:T(128)} %eo_ref.1, s32[2]{0:T(128)} %off_ref.1), custom_call_target="tpu_custom_call" | custom-call | tf_op jit(solution)/shard_map/pair_amplitudes/pallas_call | solution.py:359
  47.5 1.7 %copy.6 = f32[1,512,128]{2,1,0:T(8,128)} copy(f32[1,512,128]{2,1,0:T(8,128)} %pair_amplitudes.1) | data formatting | bytes 524288

commit v4 on v3

--- a/solution.py
+++ b/solution.py
@@ -17,8 +17,12 @@
 
 
 def row_of(g, par, kind, sgn, c):
-    if g in (0, 4):
-        entry = (0 if g == 0 else 28) + kind * 2 + par
+    if g == 0:
+        entry = kind * 2 + par
+    elif g == 4:
+        entry = 24 + par * 4 + 2 + kind
+    elif g == 3 and kind == 1:
+        entry = 24 + par * 4 + sgn
     else:
         entry = 4 + (g - 1) * 8 + kind * 4 + par * 2 + sgn
     return entry * 64 + PIECE * c
@@ -59,7 +63,7 @@
 N_COPIES = 176
 
 
-def kernel(b_ref, ev_ref, eo_ref, off_ref, out_ref, g_ref, inv_ref, ct_ref, w_ref, evc_ref, amp_ref,
+def kernel(b_hbm, ev_hbm, eo_hbm, off_hbm, out_hbm, b_ref, ev_ref, eo_ref, off_ref, out_ref, g_ref, inv_ref, ct_ref, w_ref, evc_ref, amp_ref,
            acc_ref, sb_ref, offb_ref, rd_ref, rx_ref, ry_ref, t3_ref, ry2_ref, t2_ref, rx2_ref, send_sem, recv_sem, local_sem):
     blk = lax.axis_index("blk")
     rep = lax.axis_index("rep")
@@ -91,13 +95,20 @@
                 xh = other if dx else x_hi
                 peers.append((blk, xh * NY + to))
 
-    rows8 = lax.broadcasted_iota(jnp.int32, (8, 128), 0)
-    offb_ref[0] = jnp.where(rows8 == 0, off_ref[0], jnp.where(rows8 == 1, off_ref[1], -1))
+    loads = []
+    for n, (src, dst) in enumerate(((off_hbm, off_ref), (b_hbm, b_ref), (ev_hbm, ev_ref), (eo_hbm, eo_ref))):
+        loads.append(pltpu.make_async_copy(src, dst, local_sem.at[1 + n]))
 
     barrier = pltpu.get_barrier_semaphore()
     greeted = (*zs, *xs, *ys[:2], sib)
     for who in greeted:
         pl.semaphore_signal(barrier, inc=1, device_id=who, device_id_type=MESH)
+    for load in loads:
+        load.start()
+    loads[0].wait()
+    rows8 = lax.broadcasted_iota(jnp.int32, (8, 128), 0)
+    offb_ref[0] = jnp.where(rows8 == 0, off_ref[0], jnp.where(rows8 == 1, off_ref[1], -1))
+    loads[1].wait()
     pl.semaphore_wait(barrier, len(greeted))
 
     copies = Copies(send_sem, recv_sem)
@@ -124,18 +135,19 @@
         src = same(g, sgn, c, count) if kind == 0 else slot(g, 0, 1, sgn, c, count)
         copies.start(("s", g, kind, sgn, c), src, slot(g, 1, kind, sgn, c, count), sib)
 
+    for n in range(2):
+        copies.start(("o", n), offb_ref.at[0], offb_ref.at[1 + n], ys[n])
     for i in range(4):
         z_send(0, 0, i)
         z_send(1, 0, 3 - i)
-        if i == 0:
-            for n in range(2):
-                copies.start(("o", n), offb_ref.at[0], offb_ref.at[1 + n], ys[n])
     for c in (0, 2):
         x_send(0, 0, c, 2)
     sib_send(0, 0, 0, 0, 4)
-    local = pltpu.make_async_copy(b_ref.at[pl.ds(mine, 64), :], slot(0, 0, 0, 0, 0, 4), local_sem)
+    local = pltpu.make_async_copy(b_ref.at[pl.ds(mine, 64), :], slot(0, 0, 0, 0, 0, 4), local_sem.at[0])
     local.start()
 
+    loads[2].wait()
+    loads[3].wait()
     lanes = lax.broadcasted_iota(jnp.int32, (1, 128), 1)
     low = lanes < 64
     ev_y = ev_ref[:, pl.ds(pl.multiple_of(128 * y, 128), 128)]
@@ -191,6 +203,19 @@
                                    preferred_element_type=F32)
             amp_ref[n % 2, rows, :] = (pair * (inv_ref[rows, cols] * weight)).astype(BF16)
 
+    def products(n):
+        cols = slice(BLOCK * n, BLOCK * n + BLOCK)
+        right = g_ref[cols, :]
+        for m in range(2):
+            rows = slice(256 * m, 256 * m + 256)
+            pair = lax.dot_general(b_ref[rows, :], right, (((1,), (1,)), ((), ())),
+                                   preferred_element_type=F32)
+            inv_ref[rows, cols] = pair * inv_ref[rows, cols]
+
+    def weighted(n):
+        cols = slice(BLOCK * n, BLOCK * n + BLOCK)
+        amp_ref[n % 2] = (inv_ref[:, cols] * w_ref[:, cols]).astype(BF16)
+
     def contract(n):
         for m in range(4):
             res = jnp.dot(amp_ref[n % 2], g_ref[BLOCK * n:BLOCK * n + BLOCK, 256 * m:256 * m + 256],
@@ -233,6 +258,8 @@
             if i % 2 == 1:
                 sib_send(g, 1, d, c // 2 * 2, 2)
 
+    copies.arrived(("o", 0))
+    copies.start(("o", 2), offb_ref.at[1], offb_ref.at[3], ys[0])
     for s in range(1, 5):
         for i in range(4 if s < 4 else 2):
             for d, c in ((0, i), (1, 3 - i)):
@@ -250,55 +277,57 @@
                     sib_send(4, 0, 0, c)
             if s == 1 and i == 1:
                 x_arrivals(0, 0)
-            if s > 1:
-                if i > 0:
-                    x_arrivals(s - 1, i - 1)
-            if i == 3 and s > 1:
+            if s in (2, 3) and i > 0:
+                x_arrivals(s - 1, i - 1)
+            if s in (2, 3) and i == 3:
                 x_arrivals(s - 1, 3)
-            if (s, i) == (1, 0):
-                copies.arrived(("o", 0))
-                copies.start(("o", 2), offb_ref.at[1], offb_ref.at[3], ys[0])
-            if (s, i) == (2, 0):
+            if (s, i) == (4, 0):
+                x_arrivals(3, 0)
+                x_arrivals(3, 1)
+            if (s, i) == (4, 1):
+                x_arrivals(3, 2)
+                x_arrivals(3, 3)
+            if (s, i) == (1, 3):
                 copies.arrived(("o", 1))
                 copies.arrived(("o", 2))
                 copies.start(("o", 3), offb_ref.at[pl.ds(0, 4)], offb_ref.at[pl.ds(4, 4)], partner)
-            if (s, i) == (2, 2):
+            if (s, i) == (2, 0):
                 sib_arrived(0, 0)
                 sib_arrived(0, 1)
                 local.wait()
+                products(0)
+            if (s, i) == (2, 2):
+                sib_arrived(1, 0)
+                products(1)
+            if (s, i) == (3, 0):
                 weigh()
-                amplitudes(0)
+                weighted(0)
                 contract(0)
-            if (s, i) == (2, 3):
-                sib_arrived(1, 0)
-                amplitudes(1)
-            if (s, i) == (3, 0):
+            if (s, i) == (3, 1):
+                weighted(1)
                 contract(1)
-            if (s, i) == (3, 1):
+            if (s, i) == (3, 2):
                 sib_arrived(1, 1)
                 amplitudes(2)
                 contract(2)
-            if (s, i) == (3, 2):
+            if (s, i) == (3, 3):
                 sib_arrived(2, 0)
                 amplitudes(3)
-            if (s, i) == (3, 3):
                 contract(3)
             if (s, i) == (4, 0):
                 sib_arrived(2, 1)
                 amplitudes(4)
+                contract(4)
             if (s, i) == (4, 1):
+                sib_arrived(3, 0)
+                amplitudes(5)
                 for d, c in ((0, 0), (1, 3), (0, 1), (1, 2)):
                     copies.arrived(("d", d, c))
                     sib_send(4, 1, 0, c)
-                for j in (1, 2, 3):
-                    x_arrivals(3, j)
-                contract(4)
-                sib_arrived(3, 0)
-                amplitudes(5)
                 contract(5)
-    sib_arrived(3, 1)
     amplitudes(6)
     contract(6)
+    sib_arrived(3, 1)
     sib_arrived(4, 0)
     sib_arrived(4, 1)
     amplitudes(7)
@@ -324,6 +353,14 @@
     for n, to in enumerate((y_r, y_l, y_o)):
         copies.start(("y2", n), t3_ref.at[to], ry2_ref.at[n], ys[n])
 
+    stores = []
+
+    def store(rows):
+        part = pl.ds(rows.start, rows.stop - rows.start)
+        copy = pltpu.make_async_copy(out_ref.at[part, :], out_hbm.at[0, part, :], local_sem.at[5 + len(stores)])
+        copy.start()
+        return copy
+
     def y_sum(which):
         total = acc_ref[which * NY + y, Y_FIRST, :]
         for n in range(3):
@@ -339,29 +376,38 @@
     for n in range(7):
         copies.arrived(("r", n))
         total = total + rd_ref[n].astype(F32)
-    out_ref[0, DIRECT, :] = total
+    out_ref[DIRECT, :] = total
+    stores.append(store(DIRECT))
     total = acc_ref[rep, X_FIRST, :] + rx_ref[y].astype(F32)
     for n in range(3):
         copies.arrived(("y2", n))
         total = total + ry2_ref[n].astype(F32)
-    out_ref[0, X_FIRST, :] = total
+    out_ref[X_FIRST, :] = total
+    stores.append(store(X_FIRST))
     total = y_sum(x_hi)
     copies.arrived(("x2", 0))
-    out_ref[0, Y_FIRST, :] = total + rx2_ref[...].astype(F32)
+    out_ref[Y_FIRST, :] = total + rx2_ref[...].astype(F32)
+    stores.append(store(Y_FIRST))
+    for copy in stores:
+        copy.wait()
     copies.finish()
 
 
 def per_device(integrals, eps_occ, eps_vir, offsets):
     v, aux = integrals.shape[1:]
     n_x, n_y, n_d = (part.stop - part.start for part in (X_FIRST, Y_FIRST, DIRECT))
-    vmem = pl.BlockSpec(memory_space=pltpu.VMEM)
-    smem = pl.BlockSpec(memory_space=pltpu.SMEM)
+    anywhere = pl.BlockSpec(memory_space=pl.ANY)
     return pl.pallas_call(
         kernel,
         out_shape=jax.ShapeDtypeStruct((1, v, aux // 8), F32),
-        in_specs=[vmem, vmem, smem, smem],
-        out_specs=vmem,
+        in_specs=[anywhere] * 4,
+        out_specs=anywhere,
         scratch_shapes=[
+            pltpu.VMEM((v, aux), BF16),
+            pltpu.VMEM((1, v), F32),
+            pltpu.SMEM((ORBS,), F32),
+            pltpu.SMEM((2,), jnp.int32),
+            pltpu.VMEM((v, aux // 8), F32),
             pltpu.VMEM((2048, aux), BF16),
             pltpu.VMEM((v, 2048), F32),
             pltpu.VMEM((1, 2048), F32),
@@ -380,10 +426,10 @@
             pltpu.VMEM((n_y, 128), BF16),
             pltpu.SemaphoreType.DMA((N_COPIES,)),
             pltpu.SemaphoreType.DMA((N_COPIES,)),
-            pltpu.SemaphoreType.DMA,
+            pltpu.SemaphoreType.DMA((8,)),
         ],
         compiler_params=pltpu.CompilerParams(
-            collective_id=0, has_side_effects=True, vmem_limit_bytes=56 << 20
+            collective_id=0, has_side_effects=True, vmem_limit_bytes=54784 << 10
         ),
         name="pair_amplitudes",
     )(integrals[0], eps_vir[None, :], eps_occ, offsets)

time: 49.3 us -> 45.1 us (0.915)
  Pallas kernels: 47.5 us -> 43.6 us
    pallas_call x1, Pallas kernels: 47.5 us -> 43.6 us  [per_device(): pl.pallas_call(kernel, out_shape=jax.ShapeDtypeStruct((1, v, aux // 8), F...]
    unnamed x1 -> x7, local copies, waits for them, and re-layouts: 1.67 us -> 1.39 us
where the time goes in v4:
time: 45.1 us; the launch traced here: 45 us
  Pallas kernels  43.6 us (97%)
  local copies, waits for them, and re-layouts  1.39 us (3%)
    pallas_call x1, Pallas kernels, per_device(): pl.pallas_call(kernel, out_shape=jax.ShapeDtypeStruct((1, v, aux // 8), F...  43.6 us
    unnamed x7, local copies, waits for them, and re-layouts  1.39 us

profile of v4, /device:TPU:1, one launch (start us, length us, event | category | flops | bytes accessed | tf_op | source)
XLA Modules:
  0.0 45.0 jit_solution(2339814401932476768)
XLA Ops:
  0.0 0.0 copy-start
  0.0 0.0 copy-start.1
  0.0 0.0 copy-start.2
  0.0 0.7 %copy-done = f32[512]{0:T(512)S(1)} copy-done((f32[512]{0:T(512)S(1)}, f32[512]{0:T(512)}, u32[]{:S(2)}) %copy-start) | copy-done | bytes 2072
  0.7 0.0 copy-done.1
  0.7 0.0 copy-done.2
  0.7 43.6 %pair_amplitudes.1 = f32[1,512,128]{2,1,0:T(8,128)S(1)} custom-call(bf16[512,1024]{1,0:T(8,128)(2,1)} %bitcast.3, f32[1,512]{1,0:T(1,128)S(1)} %bitcast.2, f32[32]{0:T(128)S(1)} %copy-done.1, s32[2]{0:T(128)S(1)} %copy-done.2), custom_call_target="tpu_custom_call" | custom-call | tf_op jit(solution)/shard_map/pair_amplitudes/pallas_call | solution.py:400
  44.3 0.7 %copy.6 = f32[1,512,128]{2,1,0:T(8,128)} copy(f32[1,512,128]{2,1,0:T(8,128)S(1)} %pair_amplitudes.1) | data formatting | bytes 524288
Async XLA Ops:
  0.0 0.7 %copy-start = (f32[512]{0:T(512)S(1)}, f32[512]{0:T(512)}, u32[]{:S(2)}) copy-start(f32[512]{0:T(512)} %param.6) | copy-start | bytes 6148
  0.0 0.7 %copy-start.1 = (f32[32]{0:T(128)S(1)}, f32[32]{0:T(128)}, u32[]{:S(2)}) copy-start(f32[32]{0:T(128)} %eo_hbm.1) | copy-start | bytes 388
  0.0 0.7 %copy-start.2 = (s32[2]{0:T(128)S(1)}, s32[2]{0:T(128)}, u32[]{:S(2)}) copy-start(s32[2]{0:T(128)} %off_hbm.1) | copy-start | bytes 28

commit v5 on v4

--- a/solution.py
+++ b/solution.py
@@ -11,31 +11,19 @@
 
 NZ, NY, NX = 8, 4, 4
 ORBS = 32
-PIECE = 16
+PIECE = 32
 BLOCK = 256
 X_FIRST, Y_FIRST, DIRECT = slice(0, 192), slice(192, 384), slice(384, 512)
 
 
-def row_of(g, par, kind, sgn, c):
+def row_of(g, rel, kind, par, q):
+    if g == 4:
+        return 1664 + 256 * rel + (kind * 2 + par) * PIECE
     if g == 0:
-        entry = kind * 2 + par
-    elif g == 4:
-        entry = 24 + par * 4 + 2 + kind
-    elif g == 3 and kind == 1:
-        entry = 24 + par * 4 + sgn
-    else:
-        entry = 4 + (g - 1) * 8 + kind * 4 + par * 2 + sgn
-    return entry * 64 + PIECE * c
-
-
-def entry_list():
-    out = [None] * 32
-    for g in range(5):
-        for par in range(2):
-            for kind in range(2):
-                for sgn in range(1 if g in (0, 4) else 2):
-                    out[row_of(g, par, kind, sgn, 0) // 64] = (par, kind, g if sgn else -g)
-    return out
+        return (kind * 2 + par) * 64 + PIECE * q
+    if g == 3 and kind == 1:
+        return 1536 + 256 * rel + 64 * par + PIECE * q
+    return (4 + (g - 1) * 8 + kind * 4 + rel * 2 + par) * 64 + PIECE * q
 
 
 class Copies:
@@ -43,11 +31,12 @@
         self.send_sem, self.recv_sem = send_sem, recv_sem
         self.made = {}
 
-    def start(self, name, src, dst, device):
+    def start(self, name, src, dst, device, recv=None):
         n = len(self.made)
         copy = pltpu.make_async_remote_copy(
             src_ref=src, dst_ref=dst, send_sem=self.send_sem.at[n],
-            recv_sem=self.recv_sem.at[n], device_id=device, device_id_type=MESH,
+            recv_sem=self.recv_sem.at[n + 4 if recv is None else recv],
+            device_id=device, device_id_type=MESH,
         )
         self.made[name] = copy
         copy.start()
@@ -55,12 +44,12 @@
     def arrived(self, name):
         self.made[name].wait_recv()
 
-    def finish(self):
-        for copy in self.made.values():
-            copy.wait_send()
-
-
-N_COPIES = 176
+    def finish(self, names):
+        for name in names:
+            self.made[name].wait_send()
+
+
+N_COPIES = 112
 
 
 def kernel(b_hbm, ev_hbm, eo_hbm, off_hbm, out_hbm, b_ref, ev_ref, eo_ref, off_ref, out_ref, g_ref, inv_ref, ct_ref, w_ref, evc_ref, amp_ref,
@@ -80,9 +69,12 @@
 
     x_r, x_l = lax.rem(x + 1, NX), lax.rem(x + NX - 1, NX)
     z_r, z_l = lax.rem(z + 1, NZ), lax.rem(z + NZ - 1, NZ)
-    zs = (device(x, z_r, core), device(x, z_l, core))
     xs = (device(x_r, z, core), device(x_l, z, core))
-    diagonal = (device(x_r, z_r, core), device(x_l, z_l, core))
+    z_f = lax.rem(z + 1 + (NZ - 2) * core, NZ)
+    onward = device(x, z_f, core)
+    x_f, x_s = lax.rem(x + 1 + 2 * core, NX), lax.rem(x + 3 - 2 * core, NX)
+    sideways = (device(x_f, z, core), device(x_s, z, core))
+    diagonal = device(x_f, z_f, core)
     sib = device(x, z, 1 - core)
     y_r, y_l, y_o = lax.rem(y + 1, NY), lax.rem(y + NY - 1, NY), lax.rem(y + 2, NY)
     ys = ((blk, x_hi * NY + y_r), (blk, x_hi * NY + y_l), (blk, x_hi * NY + y_o))
@@ -100,7 +92,8 @@
         loads.append(pltpu.make_async_copy(src, dst, local_sem.at[1 + n]))
 
     barrier = pltpu.get_barrier_semaphore()
-    greeted = (*zs, *xs, *ys[:2], sib)
+    around = [device(x, zz, cc) for zz in (z_r, z_l) for cc in (0, 1)]
+    greeted = (*around, *xs, *ys[:2], sib)
     for who in greeted:
         pl.semaphore_signal(barrier, inc=1, device_id=who, device_id_type=MESH)
     for load in loads:
@@ -114,64 +107,83 @@
     copies = Copies(send_sem, recv_sem)
     mine = pl.multiple_of(128 * y + 64 * x_hi, 64)
 
-    def slot(g, par, kind, sgn, c, count=1):
-        return g_ref.at[pl.ds(row_of(g, par, kind, sgn, c), PIECE * count), :]
-
-    def same(g, sgn, c, count=1):
-        if g == 0:
-            return b_ref.at[pl.ds(mine + PIECE * c, PIECE * count), :]
-        return slot(g, 0, 0, sgn, c, count)
-
-    def sign(g, d):
-        return 0 if g in (0, 4) else d
-
-    def z_send(d, s, c):
-        copies.start(("z", d, s, c), same(s, sign(s, d), c), slot(s + 1, 0, 0, sign(s + 1, d), c), zs[d])
-
-    def x_send(g, sgn, c, count=1):
-        copies.start(("x", g, sgn, c), same(g, sgn, c, count), slot(g, 0, 1, sgn, c, count), xs[c // 2])
-
-    def sib_send(g, kind, sgn, c, count=1):
-        src = same(g, sgn, c, count) if kind == 0 else slot(g, 0, 1, sgn, c, count)
-        copies.start(("s", g, kind, sgn, c), src, slot(g, 1, kind, sgn, c, count), sib)
+    def half(i):
+        return i + core * (1 - 2 * i)
+
+    def slot(g, rel, kind, par, q, rows=PIECE):
+        start = row_of(g, rel, kind, par, q)
+        return g_ref.at[pl.ds(start if isinstance(start, int) else pl.multiple_of(start, PIECE), rows), :]
+
+    def own(q, rows=PIECE):
+        return b_ref.at[pl.ds(mine + PIECE * q, rows), :]
+
+    def z_send(s, par, i):
+        copies.start(("z", s, par, i), slot(s, 0, 0, par, half(i)), slot(s + 1, 0, 0, par, half(i)), onward)
+
+    def x_send(s, par, i):
+        copies.start(("x", s, par, i), slot(s, 0, 0, par, half(i)), slot(s, 0, 1, par, half(i)), sideways[i])
+
+    def sib_send(g, kind, par, i):
+        copies.start(("s", g, kind, par, i), slot(g, 0, kind, par, half(i)), slot(g, 1, kind, par, half(i)), sib)
 
     for n in range(2):
         copies.start(("o", n), offb_ref.at[0], offb_ref.at[1 + n], ys[n])
-    for i in range(4):
-        z_send(0, 0, i)
-        z_send(1, 0, 3 - i)
-    for c in (0, 2):
-        x_send(0, 0, c, 2)
-    sib_send(0, 0, 0, 0, 4)
-    local = pltpu.make_async_copy(b_ref.at[pl.ds(mine, 64), :], slot(0, 0, 0, 0, 0, 4), local_sem.at[0])
+    for i in range(2):
+        for d, to in enumerate((device(x, z_r, 0), device(x, z_l, 1))):
+            q = 1 - i if d else i
+            copies.start(("z", 0, d, i), own(q), slot(1, 0, 0, core, q), to, recv=core * 2 + i)
+    for q in range(2):
+        copies.start(("x", 0, q), own(q), slot(0, 0, 1, 0, q), xs[q])
+    copies.start(("s", 0, 0), own(0, 64), slot(0, 0, 0, 1, 0, 64), sib)
+    local = pltpu.make_async_copy(own(0, 64), slot(0, 0, 0, 0, 0, 64), local_sem.at[0])
     local.start()
 
     loads[2].wait()
     loads[3].wait()
     lanes = lax.broadcasted_iota(jnp.int32, (1, 128), 1)
-    low = lanes < 64
     ev_y = ev_ref[:, pl.ds(pl.multiple_of(128 * y, 128), 128)]
-    ev_swap = jnp.concatenate([ev_y[:, 64:], ev_y[:, :64]], axis=1)
+    turned = [ev_y] + [jnp.concatenate([ev_y[:, 32 * t:], ev_y[:, :32 * t]], axis=1) for t in (1, 2, 3)]
+    chunk = lax.div(lanes, PIECE)
     e_k = eo_ref[blk]
-    half_of_lane = lax.div(lanes, 64)
-    quarter = lax.rem(lax.div(lanes, 32), 2)
-    half_flip = jnp.where(quarter == 0, lax.div(x_l, 2), lax.div(x_r, 2))
+    from_left, from_right = 2 * lax.div(x_l, 2), 2 * lax.div(x_r, 2) + 1
+
+    def orbital(kind, dz, par):
+        xl = x_lo if kind == 0 else 1 - x_lo
+        return xl * (2 * NZ) + lax.rem(z + dz + NZ, NZ) * 2 + par
+
+    runs = [None] * 64
+    for kind in range(2):
+        quarters = (2 * x_hi, 2 * x_hi + 1) if kind == 0 else (from_left, from_right)
+        for rel in range(2):
+            toward = 2 * core - 1 if rel == 0 else 1 - 2 * core
+            for par in range(2):
+                for g in (1, 2, 3):
+                    for q in range(2):
+                        runs[row_of(g, rel, kind, par, q) // PIECE] = (orbital(kind, g * toward, par), quarters[q])
+                q = core if rel == 0 else 1 - core
+                runs[row_of(4, rel, kind, par, 0) // PIECE] = (
+                    orbital(kind, 4, par), quarters[0] + q * (quarters[1] - quarters[0]))
+        for par in range(2):
+            for q in range(2):
+                runs[row_of(0, 0, kind, par, q) // PIECE] = (
+                    orbital(kind, 0, core if par == 0 else 1 - core), quarters[q])
+
+    def by_chunk(values):
+        first = jnp.where(chunk == 0, values[0], values[1])
+        return jnp.where(chunk < 2, first, jnp.where(chunk == 2, values[2], values[3]))
+
     distances = []
-    ents = entry_list()
-    for n in range(0, 32, 2):
-        e_l, dist, half = [], [], []
-        for par, kind, dz in ents[n:n + 2]:
-            c = core if par == 0 else 1 - core
-            xl = x_lo if kind == 0 else 1 - x_lo
-            orb = xl * (2 * NZ) + lax.rem(z + dz + NZ, NZ) * 2 + c
+    for n in range(0, 64, 4):
+        e_l, dist, turn = [], [], []
+        for place, (orb, quarter) in enumerate(runs[n:n + 4]):
             gap = lax.rem(blk - orb + ORBS, ORBS)
             e_l.append(eo_ref[orb])
             dist.append(jnp.minimum(gap, ORBS - gap))
-            half.append(jnp.full((1, 128), x_hi, jnp.int32) if kind == 0 else half_flip)
-        want = jnp.where(low, half[0], half[1])
-        ev_b = jnp.where(want == half_of_lane, ev_y, ev_swap)
-        ct_ref[:, 64 * n:64 * n + 128] = ev_b - e_k - jnp.where(low, e_l[0], e_l[1])
-        distances.append((64 * n, jnp.where(low, dist[0], dist[1])))
+            turn.append(lax.rem(quarter + 4 - place, 4))
+        turn = by_chunk(turn)
+        ev_b = jnp.where(turn == 0, turned[0], jnp.where(turn == 1, turned[1], jnp.where(turn == 2, turned[2], turned[3])))
+        ct_ref[:, PIECE * n:PIECE * n + 128] = ev_b - e_k - by_chunk(e_l)
+        distances.append((PIECE * n, by_chunk(dist)))
     for n in range(4):
         tile = jnp.broadcast_to(ev_ref[:, 128 * n:128 * n + 128], (128, 128))
         evc_ref[128 * n:128 * n + 128, :] = tile.T
@@ -193,12 +205,11 @@
             count = jnp.sum(jnp.where(table == dist, 1.0, 0.0), axis=0, keepdims=True)
             w_ref[:, col:col + 128] = jnp.where(dist == 0, 2.0 * count, count)
 
-    def amplitudes(n):
+    def amplitudes(n, parts=(slice(0, 256), slice(256, 512))):
         cols = slice(BLOCK * n, BLOCK * n + BLOCK)
         right = g_ref[cols, :]
         weight = w_ref[:, cols]
-        for m in range(2):
-            rows = slice(256 * m, 256 * m + 256)
+        for rows in parts:
             pair = lax.dot_general(b_ref[rows, :], right, (((1,), (1,)), ((), ())),
                                    preferred_element_type=F32)
             amp_ref[n % 2, rows, :] = (pair * (inv_ref[rows, cols] * weight)).astype(BF16)
@@ -237,56 +248,51 @@
                 sb_ref[j, rows, :] = val.astype(BF16)
 
     def sib_arrived(g, kind):
-        for sgn in range(1 if g in (0, 4) else 2):
-            if g == 0 and kind == 0:
-                copies.arrived(("s", 0, 0, 0, 0))
-            elif g == 4:
-                for c in range(4):
-                    copies.arrived(("s", g, kind, 0, c))
-            else:
-                for c in (0, 2):
-                    copies.arrived(("s", g, kind, sgn, c))
-
-    def x_arrivals(g, i):
         if g == 0:
-            for c in (0, 2):
-                copies.arrived(("x", 0, 0, c))
-                sib_send(0, 1, 0, c, 2)
+            copies.arrived(("s", 0, kind))
             return
-        for d, c in ((0, i), (1, 3 - i)):
-            copies.arrived(("x", g, d, c))
-            if i % 2 == 1:
-                sib_send(g, 1, d, c // 2 * 2, 2)
+        for i in range(2 if g < 4 else 1):
+            for par in range(2):
+                copies.arrived(("s", g, kind, par, i))
+
+    def x_arrivals(g, j):
+        copies.arrived(("x", g, j % 2, j // 2))
+        sib_send(g, 1, j % 2, j // 2)
 
     copies.arrived(("o", 0))
     copies.start(("o", 2), offb_ref.at[1], offb_ref.at[3], ys[0])
     for s in range(1, 5):
         for i in range(4 if s < 4 else 2):
-            for d, c in ((0, i), (1, 3 - i)):
-                copies.arrived(("z", d, s - 1, c))
-                if s < 3 or (s == 3 and i < 2):
-                    z_send(d, s, c)
-                if s == 3 and i < 2:
-                    copies.start(("d", d, c), slot(3, 0, 0, d, c), slot(4, 0, 1, 0, c), diagonal[d])
-            for d, c in ((0, i), (1, 3 - i)):
-                if s < 4:
-                    x_send(s, d, c)
-                    if i % 2 == 1:
-                        sib_send(s, 0, d, c // 2 * 2, 2)
-                else:
-                    sib_send(4, 0, 0, c)
+            part, par = i // 2, i % 2
+            if s == 1:
+                piece = slot(1, 0, 0, par, half(part))
+                pltpu.make_async_remote_copy(
+                    src_ref=piece, dst_ref=piece, send_sem=send_sem.at[0], recv_sem=recv_sem.at[par * 2 + part],
+                    device_id=onward, device_id_type=MESH,
+                ).wait_recv()
+            else:
+                copies.arrived(("z", s - 1, par, part))
+            if s < 3 or (s == 3 and part == 0):
+                z_send(s, par, part)
+            if s == 3 and part == 0:
+                copies.start(("d", par), slot(3, 0, 0, par, half(0)), slot(4, 0, 1, par, 0), diagonal)
+            if s < 4:
+                x_send(s, par, part)
+            sib_send(s, 0, par, part)
             if s == 1 and i == 1:
-                x_arrivals(0, 0)
+                for q in range(2):
+                    copies.arrived(("x", 0, q))
+                copies.start(("s", 0, 1), slot(0, 0, 1, 0, 0, 64), slot(0, 0, 1, 1, 0, 64), sib)
             if s in (2, 3) and i > 0:
                 x_arrivals(s - 1, i - 1)
             if s in (2, 3) and i == 3:
                 x_arrivals(s - 1, 3)
+            if s == 4:
+                copies.arrived(("d", par))
+                sib_send(4, 1, par, 0)
             if (s, i) == (4, 0):
                 x_arrivals(3, 0)
                 x_arrivals(3, 1)
-            if (s, i) == (4, 1):
-                x_arrivals(3, 2)
-                x_arrivals(3, 3)
             if (s, i) == (1, 3):
                 copies.arrived(("o", 1))
                 copies.arrived(("o", 2))
@@ -321,31 +327,34 @@
             if (s, i) == (4, 1):
                 sib_arrived(3, 0)
                 amplitudes(5)
-                for d, c in ((0, 0), (1, 3), (0, 1), (1, 2)):
-                    copies.arrived(("d", d, c))
-                    sib_send(4, 1, 0, c)
+                x_arrivals(3, 2)
+                x_arrivals(3, 3)
                 contract(5)
     amplitudes(6)
     contract(6)
     sib_arrived(3, 1)
     sib_arrived(4, 0)
     sib_arrived(4, 1)
-    amplitudes(7)
-
+
+    gathers = list(copies.made)
     def sliced(ref, which, to, rows):
         return ref.at[which * NY + to, pl.ds(rows.start, rows.stop - rows.start), :]
 
+    amplitudes(7, (X_FIRST,))
     contract_last(other, X_FIRST)
     copies.start(("x1", 0), sb_ref.at[pl.ds(other * NY, NY), pl.ds(0, 192), :], rx_ref, partner)
+    amplitudes(7, (Y_FIRST,))
     for which in (0, 1):
         contract_last(which, Y_FIRST)
         for n, to in enumerate((y_r, y_l, y_o)):
             copies.start(("y1", n, which), sliced(sb_ref, which, to, Y_FIRST), ry_ref.at[n, which], ys[n])
+    amplitudes(7, (DIRECT,))
     for which in (0, 1):
         contract_last(which, DIRECT)
     for n, who in enumerate(peers):
         copies.start(("r", n), sb_ref.at[who[1], pl.ds(384, 128), :], rd_ref.at[n], who)
     contract_last(x_hi, X_FIRST)
+    copies.finish(gathers)
 
     copies.arrived(("x1", 0))
     for to in range(NY):
@@ -390,7 +399,7 @@
     stores.append(store(Y_FIRST))
     for copy in stores:
         copy.wait()
-    copies.finish()
+    copies.finish([name for name in copies.made if name not in gathers])
 
 
 def per_device(integrals, eps_occ, eps_vir, offsets):

time: 45.1 us -> 45.5 us (level)
  no operation moved by 1% of the time
where the time goes in v5:
time: 45.5 us; the launch traced here: 45.3 us
  Pallas kernels  43.9 us (96%)
  local copies, waits for them, and re-layouts  1.39 us (3%)
    pallas_call x1, Pallas kernels, per_device(): pl.pallas_call(kernel, out_shape=jax.ShapeDtypeStruct((1, v, aux // 8), F...  43.9 us
    unnamed x7, local copies, waits for them, and re-layouts  1.39 us

profile of v5, /device:TPU:1, one launch (start us, length us, event | category | flops | bytes accessed | tf_op | source)
XLA Modules:
  0.0 45.3 jit_solution(8276749647706717393)
XLA Ops:
  0.0 0.0 copy-start
  0.0 0.0 copy-start.1
  0.0 0.0 copy-start.2
  0.0 0.7 %copy-done = f32[512]{0:T(512)S(1)} copy-done((f32[512]{0:T(512)S(1)}, f32[512]{0:T(512)}, u32[]{:S(2)}) %copy-start) | copy-done | bytes 2072
  0.7 0.0 copy-done.1
  0.7 0.0 copy-done.2
  0.7 43.9 %pair_amplitudes.1 = f32[1,512,128]{2,1,0:T(8,128)S(1)} custom-call(bf16[512,1024]{1,0:T(8,128)(2,1)} %bitcast.3, f32[1,512]{1,0:T(1,128)S(1)} %bitcast.2, f32[32]{0:T(128)S(1)} %copy-done.1, s32[2]{0:T(128)S(1)} %copy-done.2), custom_call_target="tpu_custom_call" | custom-call | tf_op jit(solution)/shard_map/pair_amplitudes/pallas_call | solution.py:409
  44.6 0.7 %copy.6 = f32[1,512,128]{2,1,0:T(8,128)} copy(f32[1,512,128]{2,1,0:T(8,128)S(1)} %pair_amplitudes.1) | data formatting | bytes 524288
Async XLA Ops:
  0.0 0.7 %copy-start = (f32[512]{0:T(512)S(1)}, f32[512]{0:T(512)}, u32[]{:S(2)}) copy-start(f32[512]{0:T(512)} %param.6) | copy-start | bytes 6148
  0.0 0.7 %copy-start.1 = (f32[32]{0:T(128)S(1)}, f32[32]{0:T(128)}, u32[]{:S(2)}) copy-start(f32[32]{0:T(128)} %eo_hbm.1) | copy-start | bytes 388
  0.0 0.7 %copy-start.2 = (s32[2]{0:T(128)S(1)}, s32[2]{0:T(128)}, u32[]{:S(2)}) copy-start(s32[2]{0:T(128)} %off_hbm.1) | copy-start | bytes 28

commit v6 on v5

--- a/solution.py
+++ b/solution.py
@@ -13,7 +13,7 @@
 ORBS = 32
 PIECE = 32
 BLOCK = 256
-X_FIRST, Y_FIRST, DIRECT = slice(0, 192), slice(192, 384), slice(384, 512)
+X_FIRST, Y_FIRST, DIRECT = slice(0, 224), slice(224, 384), slice(384, 512)
 
 
 def row_of(g, rel, kind, par, q):
@@ -24,6 +24,10 @@
     if g == 3 and kind == 1:
         return 1536 + 256 * rel + 64 * par + PIECE * q
     return (4 + (g - 1) * 8 + kind * 4 + rel * 2 + par) * 64 + PIECE * q
+
+
+def span(rows):
+    return pl.ds(rows.start, rows.stop - rows.start)
 
 
 class Copies:
@@ -305,18 +309,18 @@
             if (s, i) == (2, 2):
                 sib_arrived(1, 0)
                 products(1)
-            if (s, i) == (3, 0):
+            if (s, i) == (2, 3):
                 weigh()
                 weighted(0)
                 contract(0)
-            if (s, i) == (3, 1):
+            if (s, i) == (3, 0):
                 weighted(1)
                 contract(1)
-            if (s, i) == (3, 2):
+            if (s, i) == (3, 1):
                 sib_arrived(1, 1)
                 amplitudes(2)
                 contract(2)
-            if (s, i) == (3, 3):
+            if (s, i) == (3, 2):
                 sib_arrived(2, 0)
                 amplitudes(3)
                 contract(3)
@@ -325,10 +329,10 @@
                 amplitudes(4)
                 contract(4)
             if (s, i) == (4, 1):
+                x_arrivals(3, 2)
+                x_arrivals(3, 3)
                 sib_arrived(3, 0)
                 amplitudes(5)
-                x_arrivals(3, 2)
-                x_arrivals(3, 3)
                 contract(5)
     amplitudes(6)
     contract(6)
@@ -338,11 +342,11 @@
 
     gathers = list(copies.made)
     def sliced(ref, which, to, rows):
-        return ref.at[which * NY + to, pl.ds(rows.start, rows.stop - rows.start), :]
+        return ref.at[which * NY + to, span(rows), :]
 
     amplitudes(7, (X_FIRST,))
     contract_last(other, X_FIRST)
-    copies.start(("x1", 0), sb_ref.at[pl.ds(other * NY, NY), pl.ds(0, 192), :], rx_ref, partner)
+    copies.start(("x1", 0), sb_ref.at[pl.ds(other * NY, NY), span(X_FIRST), :], rx_ref, partner)
     amplitudes(7, (Y_FIRST,))
     for which in (0, 1):
         contract_last(which, Y_FIRST)
@@ -352,7 +356,7 @@
     for which in (0, 1):
         contract_last(which, DIRECT)
     for n, who in enumerate(peers):
-        copies.start(("r", n), sb_ref.at[who[1], pl.ds(384, 128), :], rd_ref.at[n], who)
+        copies.start(("r", n), sb_ref.at[who[1], span(DIRECT), :], rd_ref.at[n], who)
     contract_last(x_hi, X_FIRST)
     copies.finish(gathers)
 
@@ -365,7 +369,7 @@
     stores = []
 
     def store(rows):
-        part = pl.ds(rows.start, rows.stop - rows.start)
+        part = span(rows)
         copy = pltpu.make_async_copy(out_ref.at[part, :], out_hbm.at[0, part, :], local_sem.at[5 + len(stores)])
         copy.start()
         return copy
@@ -438,10 +442,10 @@
             pltpu.SemaphoreType.DMA((8,)),
         ],
         compiler_params=pltpu.CompilerParams(
-            collective_id=0, has_side_effects=True, vmem_limit_bytes=54784 << 10
+            collective_id=0, has_side_effects=True, vmem_limit_bytes=24 << 20
         ),
         name="pair_amplitudes",
-    )(integrals[0], eps_vir[None, :], eps_occ, offsets)
+    )(*[pltpu.with_memory_space_constraint(arg, pltpu.HBM) for arg in (integrals[0], eps_vir[None, :], eps_occ, offsets)])
 
 
 def solution(mesh):

time: 45.5 us -> 44.1 us (0.969)
  local copies, waits for them, and re-layouts: 1.39 us -> 0.71 us
  Pallas kernels: 43.9 us -> 43.3 us
    unnamed x7 -> x1, local copies, waits for them, and re-layouts: 1.39 us -> 0.71 us
    pallas_call x1, Pallas kernels: 43.9 us -> 43.3 us  [per_device(): pl.pallas_call(kernel, out_shape=jax.ShapeDtypeStruct((1, v, aux // 8), F...]
where the time goes in v6:
time: 44.1 us; the launch traced here: 44 us
  Pallas kernels  43.3 us (98%)
  local copies, waits for them, and re-layouts  0.71 us (2%)
    pallas_call x1, Pallas kernels, per_device(): pl.pallas_call(kernel, out_shape=jax.ShapeDtypeStruct((1, v, aux // 8), F...  43.3 us

profile of v6, /device:TPU:1, one launch (start us, length us, event | category | flops | bytes accessed | tf_op | source)
XLA Modules:
  0.0 44.0 jit_solution(7265281401625045135)
XLA Ops:
  0.0 43.3 %pair_amplitudes.1 = f32[1,512,128]{2,1,0:T(8,128)S(1)} custom-call(bf16[512,1024]{1,0:T(8,128)(2,1)} %bitcast.2, f32[1,512]{1,0:T(1,128)} %bitcast.3, f32[32]{0:T(128)} %eo_hbm.1, s32[2]{0:T(128)} %off_hbm.1), custom_call_target="tpu_custom_call" | custom-call | tf_op jit(solution)/shard_map/pair_amplitudes/pallas_call | solution.py:413
  43.3 0.7 %copy.6 = f32[1,512,128]{2,1,0:T(8,128)} copy(f32[1,512,128]{2,1,0:T(8,128)S(1)} %pair_amplitudes.1) | data formatting | bytes 524288

commit v7 on v6

--- a/solution.py
+++ b/solution.py
@@ -231,10 +231,11 @@
         cols = slice(BLOCK * n, BLOCK * n + BLOCK)
         amp_ref[n % 2] = (inv_ref[:, cols] * w_ref[:, cols]).astype(BF16)
 
-    def contract(n):
+    def contract_two(n):
         for m in range(4):
-            res = jnp.dot(amp_ref[n % 2], g_ref[BLOCK * n:BLOCK * n + BLOCK, 256 * m:256 * m + 256],
-                          preferred_element_type=F32)
+            cols = slice(256 * m, 256 * m + 256)
+            res = sum(jnp.dot(amp_ref[k], g_ref[BLOCK * (n + k):BLOCK * (n + k + 1), cols],
+                              preferred_element_type=F32) for k in range(2))
             for h in range(2):
                 val = res[:, 128 * h:128 * h + 128]
                 if n > 0:
@@ -244,7 +245,8 @@
     def contract_last(which, rows):
         for m in range(2):
             cols = pl.ds(pl.multiple_of(which * 512 + 256 * m, 256), 256)
-            res = jnp.dot(amp_ref[1, rows, :], g_ref[7 * BLOCK:, cols], preferred_element_type=F32)
+            res = sum(jnp.dot(amp_ref[k, rows, :], g_ref[BLOCK * (6 + k):BLOCK * (7 + k), cols],
+                              preferred_element_type=F32) for k in range(2))
             for h in range(2):
                 j = which * NY + 2 * m + h
                 val = res[:, 128 * h:128 * h + 128] + acc_ref[j, rows, :]
@@ -312,30 +314,26 @@
             if (s, i) == (2, 3):
                 weigh()
                 weighted(0)
-                contract(0)
+                weighted(1)
             if (s, i) == (3, 0):
-                weighted(1)
-                contract(1)
+                contract_two(0)
             if (s, i) == (3, 1):
                 sib_arrived(1, 1)
                 amplitudes(2)
-                contract(2)
             if (s, i) == (3, 2):
                 sib_arrived(2, 0)
                 amplitudes(3)
-                contract(3)
+                contract_two(2)
             if (s, i) == (4, 0):
                 sib_arrived(2, 1)
                 amplitudes(4)
-                contract(4)
             if (s, i) == (4, 1):
                 x_arrivals(3, 2)
                 x_arrivals(3, 3)
                 sib_arrived(3, 0)
                 amplitudes(5)
-                contract(5)
+                contract_two(4)
     amplitudes(6)
-    contract(6)
     sib_arrived(3, 1)
     sib_arrived(4, 0)
     sib_arrived(4, 1)

time: 44.1 us -> 43.8 us (level)
  no operation moved by 1% of the time
where the time goes in v7:
time: 43.8 us; the launch traced here: 43.7 us
  Pallas kernels  42.9 us (98%)
  local copies, waits for them, and re-layouts  0.71 us (2%)
    pallas_call x1, Pallas kernels, per_device(): pl.pallas_call(kernel, out_shape=jax.ShapeDtypeStruct((1, v, aux // 8), F...  42.9 us

profile of v7, /device:TPU:1, one launch (start us, length us, event | category | flops | bytes accessed | tf_op | source)
XLA Modules:
  0.0 43.7 jit_solution(15600338965552158798)
XLA Ops:
  0.0 42.9 %pair_amplitudes.1 = f32[1,512,128]{2,1,0:T(8,128)S(1)} custom-call(bf16[512,1024]{1,0:T(8,128)(2,1)} %bitcast.2, f32[1,512]{1,0:T(1,128)} %bitcast.3, f32[32]{0:T(128)} %eo_hbm.1, s32[2]{0:T(128)} %off_hbm.1), custom_call_target="tpu_custom_call" | custom-call | tf_op jit(solution)/shard_map/pair_amplitudes/pallas_call | solution.py:411
  43.0 0.7 %copy.6 = f32[1,512,128]{2,1,0:T(8,128)} copy(f32[1,512,128]{2,1,0:T(8,128)S(1)} %pair_amplitudes.1) | data formatting | bytes 524288
